TPU v7x, 512 devices: a whole 4x8x8 slice. The times are simulated.
512 devices in a mesh: clip: 16 (over y_lo, z), seq: 32 (over x, y_hi, core).
Axes of the slice: x: 4, y: 8 (y_hi: 4, y_lo: 2; y = y_hi * 2 + y_lo), z: 8, core: 2. Of those that a mesh axis runs over, the one named last changes fastest.
Arguments:
- patches: bfloat16 [16, 6272, 1024], P('clip', 'seq'), may hold values from -6 to 12
- segment: int32 [16, 6272], P('clip', 'seq'), may hold values from 0 to 191, as said below
- dest_shard: int32 [16, 6144], P('clip', 'seq'), may hold values from -1 to 31, as said below
- dest_slot: int32 [16, 6144], P('clip', 'seq'), may hold values from -1 to 63, as said below
- w_qkv: bfloat16 [1024, 1536], replicated, may hold values from -1 to 4
- out_grad: bfloat16 [16, 2048, 512], P('clip', 'seq'), may hold values from -6 to 6
Outputs:
- attended: bfloat16 [16, 2048, 512], P('clip', 'seq')
- patch_grad: bfloat16 [16, 6272, 1024], P('clip', 'seq')
- weight_grad: float32 [1024, 1536], P('seq', 'clip')
Inputs may be any that keep to these rules, and one draw needn't show every extreme that they name: `segment`: within each block of 196 patches the ids start at 0, never fall and skip no value; every id names one or more patches. The number of tokens of a block is one more than its largest id. `dest_shard`: -1 exactly on the rows of a block past its number of tokens. A block of 192 rows sends at most 6 rows to each receiving block of its clip, and every receiving block gets exactly 64 rows. `dest_slot`: -1 exactly where dest_shard is -1; the rows sent to one receiving block take its rows 0 to 63 once each.
All inputs are finite; a program needn't handle non-finite values.
Results may differ from a plain program's by a relative error of at most 0.024.
Values may be sent and summed in bfloat16 or wider, within the bound.
A program may use at most 64 MiB of HBM per device.

v0:
```python
import jax
import jax.numpy as jnp
from jax import lax
from jax.sharding import PartitionSpec as P

HEADS = 8
HEAD_DIM = 64


neg_large = -1e30


def split_heads(rows_in):
    return rows_in.reshape(rows_in.shape[0], HEADS, HEAD_DIM)


def forward_fold(query_heads, running, pieces):
    scaling = HEAD_DIM ** (-0.5)
    row_max, row_total, weighted = running
    key_heads = split_heads(pieces[0])
    value_heads = split_heads(pieces[1])
    scores = (
        jnp.einsum("rhd,khd->hrk", query_heads, key_heads, preferred_element_type=jnp.float32)
        * scaling
    )
    new_max = jnp.maximum(row_max, jnp.max(scores, axis=2))
    weights = jnp.exp(scores - new_max[:, :, None])
    row_total = jnp.sum(weights, axis=2)
    weighted = jnp.einsum(
        "hrk,khd->hrd",
        weights.astype(jnp.bfloat16),
        value_heads,
        preferred_element_type=jnp.float32,
    )
    return (new_max, row_total, weighted)


def query_fold(query_heads, grad_heads, log_total, grad_dot):
    scaling = HEAD_DIM ** (-0.5)

    def combine_piece(running, pieces, offset):
        key_heads = split_heads(pieces[0])
        value_heads = split_heads(pieces[1])
        scores = (
            jnp.einsum("rhd,khd->hrk", query_heads, key_heads, preferred_element_type=jnp.float32)
            * scaling
        )
        probability = jnp.exp(scores - log_total[:, :, None])
        prob_grad = jnp.einsum(
            "rhd,khd->hrk", grad_heads, value_heads, preferred_element_type=jnp.float32
        )
        score_grad = (probability * (prob_grad - grad_dot[:, :, None])).astype(jnp.bfloat16)
        return (
            jnp.einsum("hrk,khd->hrd", score_grad, key_heads, preferred_element_type=jnp.float32)
            * scaling
        )

    return combine_piece


def key_fold(key_heads, value_heads, all_log, all_dot, pieces):
    scaling = HEAD_DIM ** (-0.5)
    piece_query = split_heads(pieces[0])
    piece_grad = split_heads(pieces[1])
    piece_log = all_log.T
    piece_dot = all_dot.T
    scores = (
        jnp.einsum("qhd,khd->hqk", piece_query, key_heads, preferred_element_type=jnp.float32)
        * scaling
    )
    probability = jnp.exp(scores - piece_log[:, :, None])
    value_grad = jnp.einsum(
        "hqk,qhd->hkd",
        probability.astype(jnp.bfloat16),
        piece_grad,
        preferred_element_type=jnp.float32,
    )
    prob_grad = jnp.einsum(
        "qhd,khd->hqk", piece_grad, value_heads, preferred_element_type=jnp.float32
    )
    score_grad = (probability * (prob_grad - piece_dot[:, :, None])).astype(jnp.bfloat16)
    key_grad = (
        jnp.einsum("hqk,qhd->hkd", score_grad, piece_query, preferred_element_type=jnp.float32)
        * scaling
    )
    return (key_grad, value_grad)


def head_rows(matrix):
    return matrix.transpose(1, 0, 2).reshape(matrix.shape[1], HEADS * HEAD_DIM)


def local(patches, segment, dest_shard, dest_slot, w_qkv, out_grad):
    shard_count = lax.axis_size("seq")
    patch_rows = patches[0]
    patch_token = segment[0]
    targets = dest_shard[0]
    slot_ids = dest_slot[0]
    token_cap = targets.shape[0]
    pair_cap = token_cap // shard_count
    local_rows = out_grad.shape[1]
    inner_width = HEADS * HEAD_DIM
    member = (
        lax.broadcasted_iota(jnp.int32, (token_cap, patch_token.shape[0]), 0)
        == patch_token[None, :]
    )
    member_half = member.astype(jnp.bfloat16)
    counts = jnp.sum(member.astype(jnp.float32), axis=1)
    token_sums = jnp.dot(member_half, patch_rows, preferred_element_type=jnp.float32)
    tokens = (token_sums / jnp.maximum(counts, 1.0)[:, None]).astype(jnp.bfloat16)
    to_shard = (
        targets[:, None] == lax.broadcasted_iota(jnp.int32, (token_cap, shard_count), 1)
    ).astype(jnp.int32)
    ranking = jnp.sum((jnp.cumsum(to_shard, axis=0) - 1) * to_shard, axis=1)
    position = jnp.where(targets >= 0, targets * pair_cap + ranking, -1)
    chooser = position[None, :] == lax.broadcasted_iota(
        jnp.int32, (shard_count * pair_cap, token_cap), 0
    )
    chooser_half = chooser.astype(jnp.bfloat16)
    send_rows = jnp.dot(chooser_half, tokens, preferred_element_type=jnp.float32).astype(
        jnp.bfloat16
    )
    send_slot = jnp.sum(chooser.astype(jnp.int32) * (slot_ids + 1)[None, :], axis=1) - 1
    came_rows, came_slot = (
        lax.all_to_all(
            send_rows.reshape(shard_count, pair_cap, -1),
            "seq",
            split_axis=0,
            concat_axis=0,
            tiled=True,
        ),
        lax.all_to_all(
            send_slot.reshape(shard_count, pair_cap), "seq", split_axis=0, concat_axis=0, tiled=True
        ),
    )
    came_slot = came_slot.reshape(-1)
    placer = (
        came_slot[None, :]
        == lax.broadcasted_iota(jnp.int32, (local_rows, shard_count * pair_cap), 0)
    ).astype(jnp.bfloat16)
    placed = jnp.dot(
        placer, came_rows.reshape(shard_count * pair_cap, -1), preferred_element_type=jnp.float32
    ).astype(jnp.bfloat16)
    projected = jnp.dot(placed, w_qkv, preferred_element_type=jnp.float32).astype(jnp.bfloat16)
    query_rows = projected[:, :inner_width]
    key_rows = projected[:, inner_width : 2 * inner_width]
    value_rows = projected[:, 2 * inner_width :]
    query_heads = split_heads(query_rows)
    initial = (
        jnp.full((HEADS, local_rows), neg_large, jnp.float32),
        jnp.zeros((HEADS, local_rows), jnp.float32),
        jnp.zeros((HEADS, local_rows, HEAD_DIM), jnp.float32),
    )
    row_max, row_total, weighted = forward_fold(
        query_heads,
        initial,
        (
            lax.all_gather(key_rows, "seq", axis=0, tiled=True),
            lax.all_gather(value_rows, "seq", axis=0, tiled=True),
        ),
    )
    attended_rows = head_rows((weighted / row_total[:, :, None]).astype(jnp.bfloat16))
    grad_rows = out_grad[0]
    grad_heads = split_heads(grad_rows)
    log_total = row_max + jnp.log(row_total)
    grad_dot = jnp.sum(
        grad_heads.astype(jnp.float32) * split_heads(attended_rows).astype(jnp.float32), axis=2
    )
    blank = jnp.zeros((HEADS, local_rows, HEAD_DIM), jnp.float32)
    query_step = query_fold(query_heads, grad_heads, log_total, grad_dot.T)
    query_grad = query_step(
        blank,
        (
            lax.all_gather(key_rows, "seq", axis=0, tiled=True),
            lax.all_gather(value_rows, "seq", axis=0, tiled=True),
        ),
        jnp.int32(0),
    )
    all_log, all_dot = (
        lax.all_gather(log_total.T, "seq", axis=0, tiled=True),
        lax.all_gather(grad_dot, "seq", axis=0, tiled=True),
    )
    key_grad, value_grad = key_fold(
        split_heads(key_rows),
        split_heads(value_rows),
        all_log,
        all_dot,
        (
            lax.all_gather(query_rows, "seq", axis=0, tiled=True),
            lax.all_gather(grad_rows, "seq", axis=0, tiled=True),
        ),
    )
    proj_grad = jnp.concatenate(
        [head_rows(query_grad), head_rows(key_grad), head_rows(value_grad)], axis=1
    ).astype(jnp.bfloat16)
    placed_grad = jnp.einsum(
        "rc,dc->rd", proj_grad, w_qkv, preferred_element_type=jnp.float32
    ).astype(jnp.bfloat16)
    partial_value = jnp.einsum(
        "rd,rc->dc", placed, proj_grad, preferred_element_type=jnp.float32
    ).astype(jnp.bfloat16)
    across = lax.psum_scatter(partial_value, "seq", scatter_dimension=0, tiled=True).astype(
        jnp.float32
    )
    weight_grad = lax.psum_scatter(
        across.astype(jnp.bfloat16), "clip", scatter_dimension=1, tiled=True
    ).astype(jnp.float32)
    back_rows = jnp.einsum(
        "rj,rd->jd", placer, placed_grad, preferred_element_type=jnp.float32
    ).astype(jnp.bfloat16)
    returned = lax.all_to_all(
        back_rows.reshape(shard_count, pair_cap, -1), "seq", split_axis=0, concat_axis=0, tiled=True
    )
    token_grad = jnp.einsum(
        "jt,jd->td",
        chooser_half,
        returned.reshape(shard_count * pair_cap, -1),
        preferred_element_type=jnp.float32,
    ).astype(jnp.bfloat16)
    patch_sums = jnp.einsum(
        "tp,td->pd", member_half, token_grad, preferred_element_type=jnp.float32
    )
    patch_count = jnp.sum(member.astype(jnp.float32) * counts[:, None], axis=0)
    patch_grad = (patch_sums / patch_count[:, None]).astype(jnp.bfloat16)
    return (attended_rows[None], patch_grad[None], weight_grad)


def solution(mesh):
    return jax.shard_map(
        local,
        mesh=mesh,
        in_specs=(
            P("clip", "seq", None),
            P("clip", "seq"),
            P("clip", "seq"),
            P("clip", "seq"),
            P(),
            P("clip", "seq", None),
        ),
        out_specs=(P("clip", "seq", None), P("clip", "seq", None), P("seq", "clip")),
        check_vma=False,
    )
```

profile of v0, /device:TPU:2, one launch (start us, length us, event | category | flops | bytes accessed | tf_op | source)
XLA Modules:
  0.0 507.5 jit_solution(14821409125250477801)
XLA Ops:
  7.9 0.9 iota_compare_fusion.11
  13.2 10.3 %all-to-all-start = ((s32[32,1,6]{2,1,0:T(1,128)}), s32[32,1,6]{2,1,0:T(1,128)S(1)}, u32[]{:S(2)}, u32[]{:S(2)}) async-start(s32[32,1,6]{2,1,0:T(1,128)} %bitcast.5), calls=%async_computation | async-start | bytes 32768 | tf_op jit(solution)/shard_map/all_to_all | solution.py:132
  23.5 0.8 convert_reduce_fusion
  25.4 1.5 convolution_convert_fusion.4
  26.9 0.9 reshape.104
  27.9 4.2 all-to-all-done
  32.0 5.7 %all-to-all-start.1 = ((bf16[32,6,1024]{2,1,0:T(8,128)(2,1)}), bf16[32,6,1024]{2,1,0:T(8,128)(2,1)}, u32[]{:S(2)}, u32[]{:S(2)}) async-start(bf16[32,6,1024]{2,1,0:T(8,128)(2,1)} %reshape.104), calls=%async_computation.1 | async-start | bytes 1048576 | tf_op jit(solution)/shard_map/all_to_all | solution.py:125
  39.1 15.6 %all-to-all-done.1 = bf16[32,6,1024]{2,1,0:T(8,128)(2,1)} async-done(((bf16[32,6,1024]{2,1,0:T(8,128)(2,1)}), bf16[32,6,1024]{2,1,0:T(8,128)(2,1)}, u32[]{:S(2)}, u32[]{:S(2)}) %all-to-all-start.1) | async-done | bytes 393248 | tf_op jit(solution)/shard_map/all_to_all | solution.py:125
  54.7 1.2 reshape.105
  60.2 1.0 reshape.106
  61.2 1.0 reshape.111
  62.2 1.6 reshape.112
  63.8 13.4 %all-gather.14.cloned.1.call-done = bf16[1,2048,512]{2,1,0:T(8,128)(2,1)} async-done(((bf16[1,64,512]{2,1,0:T(8,128)(2,1)}), bf16[1,2048,512]{2,1,0:T(8,128)(2,1)}) %all-gather.14.cloned.1.call-update) | async-done | bytes 2097168 | tf_op jit(solution)/shard_map/all_gather | solution.py:190
  77.3 3.9 copy.62
  81.2 56.0 %all-gather.8.cloned.1.call-done = bf16[2048,512]{1,0:T(8,128)(2,1)} async-done(((bf16[64,512]{1,0:T(8,128)(2,1)}), bf16[2048,512]{1,0:T(8,128)(2,1)}) %all-gather.8.cloned.1.call-update) | async-done | bytes 2097168 | tf_op jit(solution)/shard_map/all_gather | solution.py:158
  137.3 3.9 copy.53
  141.2 56.1 %all-gather.10.cloned.1.call-done = bf16[2048,512]{1,0:T(8,128)(2,1)} async-done(((bf16[64,512]{1,0:T(8,128)(2,1)}), bf16[2048,512]{1,0:T(8,128)(2,1)}) %all-gather.10.cloned.1.call-update) | async-done | bytes 2097168 | tf_op jit(solution)/shard_map/all_gather | solution.py:159
  197.3 4.0 copy.55
  201.2 2.4 multiply_reduce_fusion
  203.6 0.8 fusion.2
  205.1 1.6 copy-done.4
  206.7 1.6 multiply_reduce_fusion.1
  208.3 5.2 %fusion.28 = bf16[64,8,64]{2,0,1:T(8,128)(2,1)S(1)} fusion(bf16[2048,8,64]{0,2,1:T(8,128)(2,1)} %bitcast.106, f32[8,64,2048]{2,1,0:T(8,128)} %copy-done.1, bf16[2048,8,64]{0,2,1:T(8,128)(2,1)} %bitcast.107, bf16[64,8,64]{0,2,1:T(8,128)(2,1)S(1)} %bitcast.114, f32[8,64]{1,0:T(8,128)S(1)} %bitcast.120, f32[8,64]{1,0:T(8,128)} %log_add_fusion), kind=kOutput, calls=%fused_computation.36 | convolution fusion | flops 273743872 | bytes 8523776 | tf_op jit(solution)/shard_map/hrk,khd->hrd/dot_general | solution.py:54
  213.7 0.8 reshape.109
  214.5 38.9 %all-gather.2 = f32[32,64,8]{1,2,0:T(8,128)S(1)} all-gather(f32[1,64,8]{1,2,0:T(8,128)S(1)} %bitcast.121), channel_id=1, replica_groups=mesh['clip'=16,'seq'=32] {'seq'}, dimensions={0}, use_global_device_ids=true | all-gather | bytes 67584 | tf_op jit(solution)/shard_map/all_gather | solution.py:181
  254.2 40.2 %all-gather.1 = f32[32,64,8]{1,2,0:T(8,128)S(1)} all-gather(f32[1,64,8]{1,2,0:T(8,128)S(1)} %fusion.58), channel_id=1, replica_groups=mesh['clip'=16,'seq'=32] {'seq'}, dimensions={0}, use_global_device_ids=true | all-gather | bytes 67584 | tf_op jit(solution)/shard_map/all_gather | solution.py:180
  294.5 0.8 constant_dynamic-update-slice_fusion.2
  295.4 4.0 copy.59
  299.3 2.4 fusion.44
  301.8 2.0 fusion.30
  303.8 5.9 %fusion.29 = bf16[64,8,64]{2,0,1:T(8,128)(2,1)} fusion(bf16[2048,8,64]{0,2,1:T(8,128)(2,1)} %bitcast.104, f32[8,2048,64]{1,2,0:T(8,128)} %copy-done.2, bf16[2048,8,64]{0,2,1:T(8,128)(2,1)} %bitcast.101, f32[8,2048]{1,0:T(8,128)} %bitcast.115, f32[8,2048]{1,0:T(8,128)S(1)} %bitcast.111, bf16[64,8,64]{2,1,0:T(8,128)(2,1)} %reshape.112), kind=kOutput, calls=%fused_computation.37 | convolution fusion | flops 273743872 | bytes 8650752 | tf_op jit(solution)/shard_map/hqk,qhd->hkd/dot_general | solution.py:83
  309.6 1.6 copy.65
  311.3 1.1 reshape.114
  312.3 1.6 copy.66
  314.0 1.7 reshape.115
  315.7 0.8 constant_dynamic-update-slice_fusion
  316.5 2.6 convolution_convert_fusion
  319.2 2.2 convolution_convert_fusion.3
  321.4 0.9 reshape.116
  322.3 10.2 %all-to-all-start.2 = ((bf16[32,6,1024]{2,1,0:T(8,128)(2,1)}), bf16[32,6,1024]{2,1,0:T(8,128)(2,1)}, u32[]{:S(2)}, u32[]{:S(2)}) async-start(bf16[32,6,1024]{2,1,0:T(8,128)(2,1)} %reshape.116), calls=%async_computation.2 | async-start | bytes 1048576 | tf_op jit(solution)/shard_map/all_to_all | solution.py:211
  332.7 1.6 copy.67
  334.4 13.7 %all-to-all-done.2 = bf16[32,6,1024]{2,1,0:T(8,128)(2,1)} async-done(((bf16[32,6,1024]{2,1,0:T(8,128)(2,1)}), bf16[32,6,1024]{2,1,0:T(8,128)(2,1)}, u32[]{:S(2)}, u32[]{:S(2)}) %all-to-all-start.2) | async-done | bytes 393248 | tf_op jit(solution)/shard_map/all_to_all | solution.py:211
  348.0 1.2 reshape.117
  349.2 74.2 %reduce-scatter.5.cloned.1.call-done = bf16[32,1536]{1,0:T(8,128)(2,1)} async-done(((bf16[1024,1536]{1,0:T(8,128)(2,1)}), bf16[32,1536]{1,0:T(8,128)(2,1)}) %reduce-scatter.5.cloned.1.call-update) | async-done | bytes 98320 | tf_op jit(solution)/shard_map/reduce_scatter | solution.py:202
  423.4 1.8 copy.69
  425.3 1.3 fusion.17
  426.5 72.7 %reduce-scatter.7.cloned.1.call-done = bf16[96,32]{1,0:T(8,128)(2,1)} async-done(((bf16[1536,32]{1,0:T(8,128)(2,1)}), bf16[96,32]{1,0:T(8,128)(2,1)}) %reduce-scatter.7.cloned.1.call-update) | async-done | bytes 6160
  499.3 0.8 copy.70
  (73 shorter events, 14.3 us)
Async XLA Ops:
  7.2 49.6 %copy-start = (bf16[1024,1536]{1,0:T(8,128)(2,1)S(1)}, bf16[1024,1536]{1,0:T(8,128)(2,1)}, u32[]{:S(2)}) copy-start(bf16[1024,1536]{1,0:T(8,128)(2,1)} %param.10) | copy-start | bytes 9437188
  7.2 70.1 %all-gather.14.cloned.1.call-start = ((), (), s32[]{:S(2)}) async-start(), calls=%async_computation.9 | async-start | bytes 2162688 | tf_op jit(solution)/shard_map/all_gather | solution.py:190
  11.8 0.6 copy-start.12
  13.2 18.8 %all-to-all-start = ((s32[32,1,6]{2,1,0:T(1,128)}), s32[32,1,6]{2,1,0:T(1,128)S(1)}, u32[]{:S(2)}, u32[]{:S(2)}) async-start(s32[32,1,6]{2,1,0:T(1,128)} %bitcast.5), calls=%async_computation | async-start | bytes 32768 | tf_op jit(solution)/shard_map/all_to_all | solution.py:132
  24.3 0.6 copy-start.10
  32.0 22.7 %all-to-all-start.1 = ((bf16[32,6,1024]{2,1,0:T(8,128)(2,1)}), bf16[32,6,1024]{2,1,0:T(8,128)(2,1)}, u32[]{:S(2)}, u32[]{:S(2)}) async-start(bf16[32,6,1024]{2,1,0:T(8,128)(2,1)} %reshape.104), calls=%async_computation.1 | async-start | bytes 1048576 | tf_op jit(solution)/shard_map/all_to_all | solution.py:125
  37.7 99.5 %all-gather.8.cloned.1.call-start = ((), (), s32[]{:S(2)}) async-start(), calls=%async_computation.5 | async-start | bytes 2162688 | tf_op jit(solution)/shard_map/all_gather | solution.py:158
  56.1 0.7 copy-start.5
  56.8 2.7 copy-start.8
  58.1 139.2 %all-gather.10.cloned.1.call-start = ((), (), s32[]{:S(2)}) async-start(), calls=%async_computation.6 | async-start | bytes 2162688 | tf_op jit(solution)/shard_map/all_gather | solution.py:159
  58.8 236.5 %all-gather.12.cloned.1.call-start = ((), (), s32[]{:S(2)}) async-start(), calls=%async_computation.7 | async-start | bytes 2162688 | tf_op jit(solution)/shard_map/all_gather | solution.py:189
  59.4 364.0 %reduce-scatter.5.cloned.1.call-start = ((), (), s32[]{:S(2)}) async-start(), calls=%async_computation.8 | async-start | bytes 3244032 | tf_op jit(solution)/shard_map/reduce_scatter | solution.py:202
  203.6 4.8 copy-start.1
  203.6 3.1 copy-start.4
  203.6 3.1 copy-start.9
  299.3 2.4 copy-start.3
  301.8 2.0 copy-start.2
  303.8 12.7 %copy-start.6 = (bf16[64,1024]{1,0:T(8,128)(2,1)S(1)}, bf16[64,1024]{1,0:T(8,128)(2,1)}, u32[]{:S(2)}) copy-start(bf16[64,1024]{1,0:T(8,128)(2,1)} %copy-done.5) | copy-start | bytes 393220
  316.5 2.7 copy-start.7
  319.2 13.4 %copy-start.11 = (f32[192]{0:T(256)S(1)}, f32[192]{0:T(256)}, u32[]{:S(2)}) copy-start(f32[192]{0:T(256)} %copy-done.10) | copy-start | bytes 2308
  319.2 13.4 %copy-start.14 = (s32[1,196]{1,0:T(1,128)S(1)}, s32[1,196]{1,0:T(1,128)}, u32[]{:S(2)}) copy-start(s32[1,196]{1,0:T(1,128)} %param.7) | copy-start | bytes 2356
  319.2 106.0 %copy-start.13 = (s32[1,192]{1,0:T(1,128)S(1)}, s32[1,192]{1,0:T(1,128)}, u32[]{:S(2)}) copy-start(s32[1,192]{1,0:T(1,128)} %copy-done.12) | copy-start | bytes 2308
  322.3 25.7 %all-to-all-start.2 = ((bf16[32,6,1024]{2,1,0:T(8,128)(2,1)}), bf16[32,6,1024]{2,1,0:T(8,128)(2,1)}, u32[]{:S(2)}, u32[]{:S(2)}) async-start(bf16[32,6,1024]{2,1,0:T(8,128)(2,1)} %reshape.116), calls=%async_computation.2 | async-start | bytes 1048576 | tf_op jit(solution)/shard_map/all_to_all | solution.py:211
  332.6 166.7 %reduce-scatter.7.cloned.1.call-start = ((), (), s32[]{:S(2)}) async-start(), calls=%async_computation.10 | async-start | bytes 417792
Sparse Core Ops, SparseCore 0:
  11.1 66.1 all-gather.13
  80.4 56.8 all-gather.7
  140.4 56.8 all-gather.9
  200.8 56.8 all-gather.11
  319.3 104.0 reduce-scatter.4
  426.1 73.1 reduce-scatter.6
where the time goes:
time: 509 us; the launch traced here: 508 us
  waiting for transfers between devices  308 us (61%)
  blocking collectives  79.2 us (16%)
  local copies, waits for them, and re-layouts  43.7 us (9%)
  matrix products  27.9 us (5%)
  starting transfers between devices  26.4 us (5%)
  between operations  14.4 us (3%)
  other arithmetic  8.04 us (2%)
    unnamed x7, waiting for transfers between devices  74.7 us
    reduce_scatter x1, waiting for transfers between devices, local(): lax.psum_scatter(partial_value, 'seq', scatter_dimension=0, tiled=True)  74.2 us
    all_gather x1, waiting for transfers between devices, local(): lax.all_gather(value_rows, 'seq', axis=0, tiled=True)  56.1 us
    all_gather x1, waiting for transfers between devices, local(): lax.all_gather(key_rows, 'seq', axis=0, tiled=True)  56 us
    all_gather x1, blocking collectives, local(): lax.all_gather(log_total.T, 'seq', axis=0, tiled=True)  40.2 us
    all_gather x1, blocking collectives, local(): lax.all_gather(grad_dot, 'seq', axis=0, tiled=True)  38.9 us
    all_to_all x1, waiting for transfers between devices, local(): lax.all_to_all(send_rows.reshape(shard_count, pair_cap, -1), 'seq', split...  15.6 us
    all_to_all x1, waiting for transfers between devices, local(): lax.all_to_all(back_rows.reshape(shard_count, pair_cap, -1), 'seq', split...  13.7 us
  transfers between devices with their start and end apart: 9, of which 8 were waited for; matrix products, arithmetic and copies ran while one was open for 10% of the time, Pallas kernels for 0%

commit v1 on v0

v1 whole, which is shorter than its diff:
```python
import functools

import jax
import jax.numpy as jnp
from jax import lax
from jax.experimental import pallas as pl
from jax.experimental.pallas import tpu as pltpu
from jax.sharding import PartitionSpec as P

BF = jnp.bfloat16
F32 = jnp.float32
I32 = jnp.int32
MESH = pl.DeviceIdType.MESH

D = 1024
INNER = 512
R = 64
NSEQ = 32
CAP = 8
NMSG = NSEQ * CAP
QROWS = 512
QC = 256


def iota(shape, dim):
    return lax.broadcasted_iota(I32, shape, dim)


def onehot(cond):
    return jnp.where(cond, 1.0, 0.0).astype(BF)


def mm(a, b):
    return jnp.dot(a, b, preferred_element_type=F32)


def mm_nt(a, b):
    return lax.dot_general(a, b, (((1,), (1,)), ((), ())), preferred_element_type=F32)


def mm_tn(a, b):
    return lax.dot_general(a, b, (((0,), (0,)), ((), ())), preferred_element_type=F32)


def half_lanes(shape):
    return iota(shape, len(shape) - 1) < 64


def swap(v):
    return pltpu.roll(v, 64, v.ndim - 1)


def merge_low(a, b):
    return jnp.where(half_lanes(a.shape), a, swap(b))


def merge_high(a, b):
    return jnp.where(half_lanes(a.shape), swap(a), b)


def kernel(
    n_clip,
    patches,
    segment,
    dest_shard,
    dest_slot,
    w_hbm,
    out_grad,
    att_out,
    patch_out,
    weight_out,
    send,
    recv,
    back_send,
    back_recv,
    w_all,
    w_head,
    picker,
    placer_ref,
    count_inv,
    pq,
    kv,
    kvt,
    qpad,
    dopad,
    dot_ref,
    do_send,
    do_recv,
    weights,
    part_out,
    stat_max,
    stat_sum,
    fac_ref,
    gd_ref,
    att_send,
    att_recv,
    dkv_acc,
    dq_acc,
    rs_send,
    rs_recv,
    rs_send2,
    rs_recv2,
    g_send,
    g_recv,
    gnat,
    wblk,
    ws_send,
    ws_recv,
    ws_send2,
    ws_recv2,
    w15_send,
    w15_recv,
    w2_send,
    w2_recv,
    w_sem,
    a_s,
    a_r,
    b_s,
    b_r,
    p_s,
    p_r,
    k_s,
    k_r,
    do_s,
    do_r,
    at_s,
    at_r,
    rs_s,
    rs_r,
    g_s,
    g_r,
    ws_s,
    ws_r,
    w15_s,
    w15_r,
    w2_s,
    w2_r,
):
    i = lax.axis_index("seq")
    j = lax.axis_index("clip")
    x = i // 8
    y = (i // 2) % 4
    c = i % 2
    g = i % 8
    xp, xm, x2 = (x + 1) % 4, (x + 3) % 4, (x + 2) % 4
    yp, ym, y2 = (y + 1) % 4, (y + 3) % 4, (y + 2) % 4

    def seq_dev(dx, dy, dc):
        return {"seq": dx * 8 + dy * 2 + dc}

    def rcopy(src, dst, ss, rs, dev):
        return pltpu.make_async_remote_copy(
            src_ref=src, dst_ref=dst, send_sem=ss, recv_sem=rs, device_id=dev, device_id_type=MESH
        )

    barrier = pltpu.get_barrier_semaphore()

    @pl.loop(1, NSEQ)
    def _(k):
        pl.semaphore_signal(
            barrier, inc=1, device_id={"seq": (i + k) % NSEQ}, device_id_type=MESH
        )

    @pl.loop(1, n_clip)
    def _(k):
        pl.semaphore_signal(
            barrier, inc=1, device_id={"clip": (j + k) % n_clip}, device_id_type=MESH
        )

    w_copy = pltpu.make_async_copy(w_hbm, w_all, w_sem)
    w_copy.start()

    seg = segment[...]
    tgt = dest_shard[...]
    slot = dest_slot[...]
    hit = iota((192, 196), 0) == seg
    member = onehot(hit)
    counts = jnp.sum(jnp.where(hit, 1.0, 0.0), axis=1, keepdims=True)
    sums = mm(member, patches[0])
    tokens = (sums * (1.0 / jnp.maximum(counts, 1.0))).astype(BF)
    to_shard = iota((NSEQ, 192), 0) == tgt
    shard_hot = onehot(to_shard)
    earlier = onehot(iota((192, 192), 0) < iota((192, 192), 1))
    before = mm(shard_hot, earlier)
    rank = jnp.sum(jnp.where(to_shard, before, 0.0), axis=0, keepdims=True)
    position = jnp.where(tgt >= 0, tgt.astype(F32) * CAP + rank, -1.0)
    chooser = onehot(iota((NMSG, 192), 0).astype(F32) == position)
    slot_rows = jnp.where(
        iota((128, 192), 0).astype(F32) == rank, slot.astype(F32) + 1.0, 0.0
    ).astype(BF)
    slot_table = mm_nt(shard_hot, slot_rows).astype(BF)
    spread = onehot(iota((NMSG, NSEQ), 0) == iota((NMSG, NSEQ), 1) * CAP + 6)
    slot_cells = mm(spread, slot_table)
    rows = mm(chooser, tokens)
    send[:, :, 0:128] = (rows[:, 0:128] + slot_cells).reshape(NSEQ, CAP, 128).astype(BF)
    send[:, :, 128:] = rows[:, 128:].reshape(NSEQ, CAP, D - 128).astype(BF)

    pl.semaphore_wait(barrier, NSEQ - 1 + n_clip - 1)

    def token_copy(k, peer, lands):
        return rcopy(send.at[peer], recv.at[lands], a_s.at[k], a_r.at[k], {"seq": peer})

    @pl.loop(1, NSEQ)
    def _(k):
        token_copy(k, (i + k) % NSEQ, i).start()

    recv[i] = send[i]

    picker[...] = mm(chooser, member).astype(BF)
    per_patch = mm_tn(member, jnp.broadcast_to(counts, (192, 128)).astype(BF))
    count_inv[...] = 1.0 / per_patch
    for blk in range(4):
        pair = out_grad[0, :, blk * 128 : blk * 128 + 128].astype(F32)
        top, low = pair[0:32], pair[32:64]
        do_send[2 * blk] = merge_low(top, low).astype(BF)
        do_send[2 * blk + 1] = merge_high(top, low).astype(BF)
    w_copy.wait()
    lane0 = pl.multiple_of(y * 128, 128)
    w_q = w_all[:, pl.ds(lane0, 128)].astype(F32)
    w_k = w_all[:, pl.ds(pl.multiple_of(lane0 + 512, 128), 128)].astype(F32)
    w_v = w_all[:, pl.ds(pl.multiple_of(lane0 + 1024, 128), 128)].astype(F32)
    low_half = half_lanes((D, 128))
    first = c == 0
    k_low = jnp.where(first, w_k, swap(w_k))
    v_high = jnp.where(first, swap(w_v), w_v)
    q_low = jnp.where(first, w_q, swap(w_q))
    w_head[:, 0:128] = jnp.where(low_half, k_low, v_high).astype(BF)
    w_head[:, 128:256] = jnp.where(low_half, q_low, 0.0).astype(BF)

    @pl.loop(1, NSEQ)
    def _(k):
        src = (i + NSEQ - k) % NSEQ
        token_copy(k, src, src).wait_recv()

    came = recv[...].astype(F32).reshape(NMSG, D).astype(BF)
    col = iota((NMSG, NMSG), 1)
    from_row = onehot(iota((NMSG, NMSG), 0) == (col // CAP) * CAP + 6)
    slot_sq = mm_tn(came[:, 0:128], from_row)[0:8]
    slot_row = jnp.sum(
        jnp.where(iota((8, NMSG), 0) == iota((8, NMSG), 1) % CAP, slot_sq, 0.0)
        * jnp.where(iota((8, NMSG), 1) % CAP < 6, 1.0, 0.0),
        axis=0,
        keepdims=True,
    )
    placer = onehot((iota((R, NMSG), 0) + 1).astype(F32) == slot_row)
    placer_ref[...] = placer
    pq[g] = mm(placer, came).astype(BF)

    g_p, g_m, g_2 = yp * 2 + c, ym * 2 + c, y2 * 2 + c
    A, B = pl.ds(0, 32), pl.ds(32, 32)
    to_yp, to_ym, to_pal = seq_dev(x, yp, c), seq_dev(x, ym, c), seq_dev(x, y, 1 - c)

    def p_copy(n, s, half, dev):
        ref = pq.at[s] if half is None else pq.at[s, half]
        return rcopy(ref, ref, p_s.at[n], p_r.at[n], dev)

    p_copy(0, g, A, to_yp).start()
    p_copy(1, g, B, to_ym).start()
    p_copy(2, g, B, to_yp).start()
    p_copy(3, g, A, to_ym).start()
    p_copy(4, g, None, to_pal).start()
    p_copy(0, g_m, A, to_yp).wait_recv()
    p_copy(5, g_m, A, to_yp).start()
    p_copy(6, g_m, A, to_pal).start()
    p_copy(1, g_p, B, to_ym).wait_recv()
    p_copy(7, g_p, B, to_ym).start()
    p_copy(8, g_p, B, to_pal).start()
    p_copy(2, g_m, B, to_yp).wait_recv()
    p_copy(9, g_m, B, to_pal).start()
    p_copy(3, g_p, A, to_ym).wait_recv()
    p_copy(10, g_p, A, to_pal).start()
    p_copy(5, g_2, A, to_yp).wait_recv()
    p_copy(11, g_2, A, to_pal).start()
    p_copy(7, g_2, B, to_ym).wait_recv()
    p_copy(12, g_2, B, to_pal).start()
    h_p, h_m, h_2, h_g = yp * 2 + 1 - c, ym * 2 + 1 - c, y2 * 2 + 1 - c, y * 2 + 1 - c
    p_copy(4, h_g, None, to_pal).wait_recv()
    p_copy(6, h_m, A, to_pal).wait_recv()
    p_copy(8, h_p, B, to_pal).wait_recv()
    p_copy(9, h_m, B, to_pal).wait_recv()
    p_copy(10, h_p, A, to_pal).wait_recv()
    p_copy(11, h_2, A, to_pal).wait_recv()
    p_copy(12, h_2, B, to_pal).wait_recv()

    proj = mm(pq[...].reshape(QROWS, D), w_head[...]).astype(BF)
    kv[x] = proj[:, 0:128]
    qpad[...] = (proj[:, 128:256].astype(F32) * 0.125).astype(BF)

    KA, KB = pl.ds(0, 256), pl.ds(256, 256)
    to_xp, to_xm = seq_dev(xp, y, c), seq_dev(xm, y, c)

    def k_copy(n, s, half, dev):
        ref = kv.at[s, half]
        return rcopy(ref, ref, k_s.at[n], k_r.at[n], dev)

    k_copy(0, x, KA, to_xp).start()
    k_copy(1, x, KB, to_xm).start()
    k_copy(2, x, KB, to_xp).start()
    k_copy(3, x, KA, to_xm).start()

    def do_copy(k, peer, lands):
        return rcopy(
            do_send.at[peer], do_recv.at[lands], do_s.at[k], do_r.at[k], {"seq": x * 8 + peer}
        )

    @pl.loop(1, 8)
    def _(k):
        do_copy(k, (g + k) % 8, g).start()

    do_recv[g] = do_send[g]

    def forward(s, n):
        kvt[n] = kv[s].astype(F32).T.astype(BF)
        for q in range(QROWS // QC):
            qs = slice(q * QC, q * QC + QC)
            scores = mm_nt(kv[s], qpad[qs, :])
            top = jnp.max(scores, axis=0, keepdims=True)
            w = jnp.exp(scores - top)
            stat_max[n, :, qs] = top
            stat_sum[n, :, qs] = jnp.sum(w, axis=0, keepdims=True)
            weights[n, :, qs] = w
            part_out[n, :, qs] = mm(kvt[n], w.astype(BF))

    forward(x, 0)
    k_copy(0, xm, KA, to_xp).wait_recv()
    k_copy(4, xm, KA, to_xp).start()
    k_copy(1, xp, KB, to_xm).wait_recv()
    k_copy(5, xp, KB, to_xm).start()
    k_copy(2, xm, KB, to_xp).wait_recv()
    forward(xm, 1)
    k_copy(3, xp, KA, to_xm).wait_recv()
    forward(xp, 2)

    @pl.loop(1, 8)
    def _(k):
        src = (g + 8 - k) % 8
        do_copy(k, src, src).wait_recv()

    d_in = do_recv[...].astype(F32)
    high = iota((8, 32, 128), 2) >= 64
    d_rows = jnp.concatenate(
        [jnp.where(high, swap(d_in), 0.0), jnp.where(high, d_in, 0.0)], axis=1
    ).reshape(QROWS, 128)
    dopad[...] = d_rows.astype(BF)
    dot_ref[...] = d_rows.T

    k_copy(4, x2, KA, to_xp).wait_recv()
    k_copy(5, x2, KB, to_xm).wait_recv()
    forward(x2, 3)

    best = jnp.maximum(
        jnp.maximum(stat_max[0], stat_max[1]), jnp.maximum(stat_max[2], stat_max[3])
    )
    facs = [jnp.exp(stat_max[n] - best) for n in range(4)]
    total = sum(facs[n] * stat_sum[n] for n in range(4))
    att_t = sum(facs[n] * part_out[n] for n in range(4)) / total
    att_half = att_t.astype(BF).astype(F32)
    gd_ref[...] = jnp.sum(att_half[64:128] * dot_ref[64:128], axis=0, keepdims=True)
    for n in range(4):
        fac_ref[n] = facs[n] / total
    att3 = att_half.T.reshape(8, R, 128)
    att_send[...] = merge_high(att3[:, 0:32], att3[:, 32:64]).astype(BF)

    def at_copy(k, peer, lands):
        return rcopy(
            att_send.at[peer], att_recv.at[lands], at_s.at[k], at_r.at[k], {"seq": x * 8 + peer}
        )

    @pl.loop(1, 8)
    def _(k):
        at_copy(k, (g + k) % 8, g).start()

    att_recv[g] = att_send[g]

    dq_acc[...] = jnp.zeros((128, QROWS), F32)

    def backward(s, n):
        for q in range(QROWS // QC):
            qs = slice(q * QC, q * QC + QC)
            prob_grad = mm_nt(kv[s], dopad[qs, :])
            prob = weights[n, :, qs] * fac_ref[n, :, qs]
            score_grad = (prob * (prob_grad - gd_ref[:, qs])).astype(BF)
            upd = mm(score_grad, qpad[qs, :]) + mm(prob.astype(BF), dopad[qs, :])
            if q == 0:
                dkv_acc[...] = upd
            else:
                dkv_acc[...] += upd
            dq_acc[:, qs] += mm(kvt[n], score_grad)

    def rs_copy(src, dst, n, dev):
        return rcopy(src, dst, rs_s.at[n], rs_r.at[n], dev)

    backward(x2, 3)
    rs_send[0] = dkv_acc[0:256].astype(BF)
    rs_send[1] = dkv_acc[256:512].astype(BF)
    rs_copy(rs_send.at[0], rs_recv.at[0], 0, to_xp).start()
    rs_copy(rs_send.at[1], rs_recv.at[1], 1, to_xm).start()
    backward(xp, 2)
    rs_copy(rs_send.at[0], rs_recv.at[0], 0, to_xp).wait_recv()
    rs_send2[0, 0:256] = (dkv_acc[0:256] + rs_recv[0].astype(F32)).astype(BF)
    rs_send2[0, 256:512] = dkv_acc[256:512].astype(BF)
    rs_copy(rs_send2.at[0], rs_recv2.at[0], 2, to_xp).start()
    backward(xm, 1)
    rs_copy(rs_send.at[1], rs_recv.at[1], 1, to_xm).wait_recv()
    rs_send2[1, 0:256] = dkv_acc[0:256].astype(BF)
    rs_send2[1, 256:512] = (dkv_acc[256:512] + rs_recv[1].astype(F32)).astype(BF)
    rs_copy(rs_send2.at[1], rs_recv2.at[1], 3, to_xm).start()
    backward(x, 0)

    dq_rows = jnp.where(half_lanes((QROWS, 128)), dq_acc[...].T * 0.125, 0.0)
    dq3 = dq_rows.reshape(8, R, 128)
    g_send[:, 64:96] = merge_low(dq3[:, 0:32], dq3[:, 32:64]).astype(BF)
    rs_copy(rs_send2.at[0], rs_recv2.at[0], 2, to_xp).wait_recv()
    rs_copy(rs_send2.at[1], rs_recv2.at[1], 3, to_xm).wait_recv()
    dkv = (dkv_acc[...] + rs_recv2[0].astype(F32) + rs_recv2[1].astype(F32)).astype(BF)
    g_send[:, 0:64] = dkv.reshape(8, R, 128)

    def g_copy(k, peer, lands):
        return rcopy(
            g_send.at[peer], g_recv.at[lands], g_s.at[k], g_r.at[k], {"seq": x * 8 + peer}
        )

    @pl.loop(1, 8)
    def _(k):
        g_copy(k, (g + k) % 8, g).start()

    g_recv[g] = g_send[g]

    grads = jnp.concatenate([dkv, dq_rows.astype(BF)], axis=1)
    w_part = mm_tn(grads, pq[...].reshape(QROWS, D))
    for q in range(4):
        wblk[q] = w_part[0:192, q * 256 : q * 256 + 256]

    def ws_copy(src, dst, n, dev):
        return rcopy(src, dst, ws_s.at[n], ws_r.at[n], dev)

    ws_send[0] = wblk[x2, 0:96].astype(BF)
    ws_send[1] = wblk[x2, 96:192].astype(BF)
    ws_copy(ws_send.at[0], ws_recv.at[0], 0, to_xp).start()
    ws_copy(ws_send.at[1], ws_recv.at[1], 1, to_xm).start()

    @pl.loop(1, 8)
    def _(k):
        src = (g + 8 - k) % 8
        at_copy(k, src, src).wait_recv()

    for blk in range(4):
        a0 = att_recv[2 * blk].astype(F32)
        a1 = att_recv[2 * blk + 1].astype(F32)
        lanes = slice(blk * 128, blk * 128 + 128)
        att_out[0, 0:32, lanes] = merge_low(a0, a1).astype(BF)
        att_out[0, 32:64, lanes] = merge_high(a0, a1).astype(BF)

    @pl.loop(1, 8)
    def _(k):
        src = (g + 8 - k) % 8
        g_copy(k, src, src).wait_recv()

    for blk in range(4):
        r0 = g_recv[2 * blk].astype(F32)
        r1 = g_recv[2 * blk + 1].astype(F32)
        q_at, k_at, v_at = blk * 128, blk * 128 + 512, blk * 128 + 1024
        gnat[0:32, q_at : q_at + 128] = merge_low(r0[64:96], r1[64:96]).astype(BF)
        gnat[32:64, q_at : q_at + 128] = merge_high(r0[64:96], r1[64:96]).astype(BF)
        gnat[:, k_at : k_at + 128] = merge_low(r0[0:64], r1[0:64]).astype(BF)
        gnat[:, v_at : v_at + 128] = merge_high(r0[0:64], r1[0:64]).astype(BF)
    placed_grad = mm_nt(gnat[...], w_all[...]).astype(BF)
    back = mm_tn(placer_ref[...], placed_grad)
    back_send[...] = back.reshape(NSEQ, CAP, D).astype(BF)

    def back_copy(k, peer, lands):
        return rcopy(
            back_send.at[peer], back_recv.at[lands], b_s.at[k], b_r.at[k], {"seq": peer}
        )

    @pl.loop(1, NSEQ)
    def _(k):
        back_copy(k, (i + k) % NSEQ, i).start()

    back_recv[i] = back_send[i]

    ws_copy(ws_send.at[0], ws_recv.at[0], 0, to_xp).wait_recv()
    ws_send2[0, 0:96] = (wblk[xp, 0:96] + ws_recv[0].astype(F32)).astype(BF)
    ws_send2[0, 96:192] = wblk[xp, 96:192].astype(BF)
    ws_copy(ws_send2.at[0], ws_recv2.at[0], 2, to_xp).start()
    ws_copy(ws_send.at[1], ws_recv.at[1], 1, to_xm).wait_recv()
    ws_send2[1, 0:96] = wblk[xm, 0:96].astype(BF)
    ws_send2[1, 96:192] = (wblk[xm, 96:192] + ws_recv[1].astype(F32)).astype(BF)
    ws_copy(ws_send2.at[1], ws_recv2.at[1], 3, to_xm).start()
    ws_copy(ws_send2.at[0], ws_recv2.at[0], 2, to_xp).wait_recv()
    ws_copy(ws_send2.at[1], ws_recv2.at[1], 3, to_xm).wait_recv()
    w_sum = wblk[x] + ws_recv2[0].astype(F32) + ws_recv2[1].astype(F32)
    w_kv = w_sum[0:128].T.reshape(8, 32, 128)
    w_qq = jnp.concatenate([w_sum[128:192], jnp.zeros((64, 256), F32)], axis=0)
    w_qq = w_qq.T.reshape(8, 32, 128)
    w15_send[:, 0:32] = w_kv.astype(BF)
    w15_send[:, 32:48] = merge_low(w_qq[:, 0:16], w_qq[:, 16:32]).astype(BF)

    def w15_copy(k, peer, lands):
        return rcopy(
            w15_send.at[peer],
            w15_recv.at[lands],
            w15_s.at[k],
            w15_r.at[k],
            {"seq": x * 8 + peer},
        )

    @pl.loop(1, 8)
    def _(k):
        w15_copy(k, (g + k) % 8, g).start()

    w15_recv[g] = w15_send[g]

    @pl.loop(1, 8)
    def _(k):
        src = (g + 8 - k) % 8
        w15_copy(k, src, src).wait_recv()

    q_blocks, k_blocks, v_blocks = [], [], []
    for blk in range(4):
        r0 = w15_recv[2 * blk].astype(F32)
        r1 = w15_recv[2 * blk + 1].astype(F32)
        q_blocks.append(
            jnp.concatenate(
                [merge_low(r0[32:48], r1[32:48]), merge_high(r0[32:48], r1[32:48])], axis=0
            )
        )
        k_blocks.append(merge_low(r0[0:32], r1[0:32]))
        v_blocks.append(merge_high(r0[0:32], r1[0:32]))
    blocks = q_blocks + k_blocks + v_blocks
    width = 3 * INNER // n_clip
    for n in range(n_clip):
        b, off = divmod(width * n, 128)
        if off == 0:
            piece = blocks[b]
        else:
            turn = 128 - off
            piece = pltpu.roll(blocks[b], turn, 1)
            if off + width > 128:
                piece = jnp.where(
                    iota((32, 128), 1) < turn, piece, pltpu.roll(blocks[b + 1], turn, 1)
                )
        w2_send[n] = piece.astype(BF)

    def w2_copy(k, peer, lands):
        return rcopy(
            w2_send.at[peer], w2_recv.at[lands], w2_s.at[k], w2_r.at[k], {"clip": peer}
        )

    @pl.loop(1, n_clip)
    def _(k):
        w2_copy(k, (j + k) % n_clip, j).start()

    w2_recv[j] = w2_send[j]

    @pl.loop(1, NSEQ)
    def _(k):
        src = (i + NSEQ - k) % NSEQ
        back_copy(k, src, src).wait_recv()

    returned = back_recv[...].astype(F32).reshape(NMSG, D).astype(BF)
    patch_rows = mm_tn(picker[...], returned)
    patch_out[0] = (patch_rows * count_inv[:, 0:1]).astype(BF)

    @pl.loop(1, n_clip)
    def _(k):
        src = (j + n_clip - k) % n_clip
        w2_copy(k, src, src).wait_recv()

    weight_out[...] = jnp.sum(w2_recv[...].astype(F32), axis=0)[:, 0:width]

    @pl.loop(1, NSEQ)
    def _(k):
        token_copy(k, (i + k) % NSEQ, i).wait_send()
        back_copy(k, (i + k) % NSEQ, i).wait_send()

    @pl.loop(1, 8)
    def _(k):
        peer = (g + k) % 8
        do_copy(k, peer, g).wait_send()
        at_copy(k, peer, g).wait_send()
        g_copy(k, peer, g).wait_send()
        w15_copy(k, peer, g).wait_send()

    @pl.loop(1, n_clip)
    def _(k):
        w2_copy(k, (j + k) % n_clip, j).wait_send()

    for n, s, half, dev in (
        (0, g, A, to_yp),
        (1, g, B, to_ym),
        (2, g, B, to_yp),
        (3, g, A, to_ym),
        (4, g, None, to_pal),
        (5, g_m, A, to_yp),
        (6, g_m, A, to_pal),
        (7, g_p, B, to_ym),
        (8, g_p, B, to_pal),
        (9, g_m, B, to_pal),
        (10, g_p, A, to_pal),
        (11, g_2, A, to_pal),
        (12, g_2, B, to_pal),
    ):
        p_copy(n, s, half, dev).wait_send()
    for n, s, half, dev in (
        (0, x, KA, to_xp),
        (1, x, KB, to_xm),
        (2, x, KB, to_xp),
        (3, x, KA, to_xm),
        (4, xm, KA, to_xp),
        (5, xp, KB, to_xm),
    ):
        k_copy(n, s, half, dev).wait_send()
    for n, dev in ((0, to_xp), (1, to_xm)):
        rs_copy(rs_send.at[n], rs_recv.at[n], n, dev).wait_send()
        rs_copy(rs_send2.at[n], rs_recv2.at[n], n + 2, dev).wait_send()
        ws_copy(ws_send.at[n], ws_recv.at[n], n, dev).wait_send()
        ws_copy(ws_send2.at[n], ws_recv2.at[n], n + 2, dev).wait_send()


def local(patches, segment, dest_shard, dest_slot, w_qkv, out_grad):
    n_clip = lax.axis_size("clip")
    v = pltpu.VMEM
    dma = pltpu.SemaphoreType.DMA
    vmem = pl.BlockSpec(memory_space=pltpu.VMEM)
    scratch = [
        v((NSEQ, CAP, D), BF),
        v((NSEQ, CAP, D), BF),
        v((NSEQ, CAP, D), BF),
        v((NSEQ, CAP, D), BF),
        v((D, 3 * INNER), BF),
        v((D, 256), BF),
        v((NMSG, 196), BF),
        v((R, NMSG), BF),
        v((196, 128), F32),
        v((8, R, D), BF),
        v((4, QROWS, 128), BF),
        v((4, 128, QROWS), BF),
        v((QROWS, 128), BF),
        v((QROWS, 128), BF),
        v((128, QROWS), F32),
        v((8, 32, 128), BF),
        v((8, 32, 128), BF),
        v((4, QROWS, QROWS), F32),
        v((4, 128, QROWS), F32),
        v((4, 1, QROWS), F32),
        v((4, 1, QROWS), F32),
        v((4, 1, QROWS), F32),
        v((1, QROWS), F32),
        v((8, 32, 128), BF),
        v((8, 32, 128), BF),
        v((QROWS, 128), F32),
        v((128, QROWS), F32),
        v((2, 256, 128), BF),
        v((2, 256, 128), BF),
        v((2, QROWS, 128), BF),
        v((2, QROWS, 128), BF),
        v((8, 96, 128), BF),
        v((8, 96, 128), BF),
        v((R, 3 * INNER), BF),
        v((4, 192, 256), F32),
        v((2, 96, 256), BF),
        v((2, 96, 256), BF),
        v((2, 192, 256), BF),
        v((2, 192, 256), BF),
        v((8, 48, 128), BF),
        v((8, 48, 128), BF),
        v((n_clip, 32, 128), BF),
        v((n_clip, 32, 128), BF),
        dma,
        dma((NSEQ,)),
        dma((NSEQ,)),
        dma((NSEQ,)),
        dma((NSEQ,)),
        dma((13,)),
        dma((13,)),
        dma((6,)),
        dma((6,)),
        dma((8,)),
        dma((8,)),
        dma((8,)),
        dma((8,)),
        dma((4,)),
        dma((4,)),
        dma((8,)),
        dma((8,)),
        dma((4,)),
        dma((4,)),
        dma((8,)),
        dma((8,)),
        dma((n_clip,)),
        dma((n_clip,)),
    ]
    return pl.pallas_call(
        functools.partial(kernel, n_clip),
        out_shape=(
            jax.ShapeDtypeStruct((1, R, INNER), BF),
            jax.ShapeDtypeStruct((1, 196, D), BF),
            jax.ShapeDtypeStruct((32, 3 * INNER // n_clip), F32),
        ),
        in_specs=[vmem, vmem, vmem, vmem, pl.BlockSpec(memory_space=pl.ANY), vmem],
        out_specs=(vmem, vmem, vmem),
        scratch_shapes=scratch,
        compiler_params=pltpu.CompilerParams(
            collective_id=0, has_side_effects=True, vmem_limit_bytes=56 * 1024 * 1024
        ),
        name="rebalance_attention",
    )(patches, segment, dest_shard, dest_slot, w_qkv, out_grad)


def solution(mesh):
    return jax.shard_map(
        local,
        mesh=mesh,
        in_specs=(
            P("clip", "seq", None),
            P("clip", "seq"),
            P("clip", "seq"),
            P("clip", "seq"),
            P(),
            P("clip", "seq", None),
        ),
        out_specs=(P("clip", "seq", None), P("clip", "seq", None), P("seq", "clip")),
        check_vma=False,
    )
```

time: 509 us -> 104 us (0.20)
  the two profiles are of different devices: /device:TPU:2 before, /device:TPU:1 now
where the time goes in v1:
time: 104 us
  Pallas kernels  98.4 us (95%)
  local copies, waits for them, and re-layouts  4.57 us (4%)
    pallas_call x1, Pallas kernels, local(): pl.pallas_call(functools.partial(kernel, n_clip), out_shape=(jax.ShapeDty...  98.4 us
    unnamed x3, local copies, waits for them, and re-layouts  4.57 us

profile of v1, /device:TPU:1, one launch (start us, length us, event | category | flops | bytes accessed | tf_op | source)
XLA Modules:
  0.0 103.6 jit_solution(11665302628856062239)
XLA Ops:
  0.6 98.4 %rebalance_attention.1 = (bf16[1,64,512]{2,1,0:T(8,128)(2,1)}, bf16[1,196,1024]{2,1,0:T(8,128)(2,1)}, f32[32,96]{1,0:T(8,128)}) custom-call(bf16[1,196,1024]{2,1,0:T(8,128)(2,1)} %patches.1, s32[1,196]{1,0:T(1,128)} %segment.1, s32[1,192]{1,0:T(1,128)} %dest_shard.1, s32[1,192]{1,0:T(1,128)} %dest_slot.1, bf16[1024,1536]{1,0:T(8,128)(2,1)} %w_hbm.1, ...), custom_call_target="tpu_custom_call" | custom-call | tf_op jit(solution)/shard_map/rebalance_attention/pallas_call | solution.py:694
  99.0 1.5 %copy.12 = bf16[1,64,512]{2,1,0:T(8,128)(2,1)} copy(bf16[1,64,512]{2,1,0:T(8,128)(2,1)} %get-tuple-element.6) | data formatting | bytes 131072
  100.5 1.8 %copy.13 = bf16[1,196,1024]{2,1,0:T(8,128)(2,1)} copy(bf16[1,196,1024]{2,1,0:T(8,128)(2,1)} %get-tuple-element.7) | data formatting | bytes 802816
  102.2 1.3 %copy.14 = f32[32,96]{1,0:T(8,128)} copy(f32[32,96]{1,0:T(8,128)} %get-tuple-element.8) | data formatting | bytes 24576

commit v2 on v1

--- a/solution.py
+++ b/solution.py
@@ -20,6 +20,9 @@
 NMSG = NSEQ * CAP
 QROWS = 512
 QC = 256
+TOP = 6
+EXT = D + 128
+HALF = D // 2
 
 
 def iota(shape, dim):
@@ -60,11 +63,19 @@
 
 def kernel(
     n_clip,
+    patches_hbm,
+    segment_hbm,
+    shard_hbm,
+    slot_hbm,
+    w_hbm,
+    grad_hbm,
+    att_hbm,
+    patch_hbm,
+    weight_hbm,
     patches,
     segment,
     dest_shard,
     dest_slot,
-    w_hbm,
     out_grad,
     att_out,
     patch_out,
@@ -74,7 +85,6 @@
     back_send,
     back_recv,
     w_all,
-    w_head,
     picker,
     placer_ref,
     count_inv,
@@ -84,8 +94,9 @@
     qpad,
     dopad,
     dot_ref,
-    do_send,
-    do_recv,
+    kv_send,
+    qd_send,
+    qd_recv,
     weights,
     part_out,
     stat_max,
@@ -112,7 +123,8 @@
     w15_recv,
     w2_send,
     w2_recv,
-    w_sem,
+    in_sem,
+    out_sem,
     a_s,
     a_r,
     b_s,
@@ -121,8 +133,10 @@
     p_r,
     k_s,
     k_r,
-    do_s,
-    do_r,
+    kx_s,
+    kx_r,
+    qd_s,
+    qd_r,
     at_s,
     at_r,
     rs_s,
@@ -153,6 +167,22 @@
             src_ref=src, dst_ref=dst, send_sem=ss, recv_sem=rs, device_id=dev, device_id_type=MESH
         )
 
+    loads = [
+        pltpu.make_async_copy(a, b, in_sem.at[n])
+        for n, (a, b) in enumerate(
+            (
+                (segment_hbm, segment),
+                (shard_hbm, dest_shard),
+                (slot_hbm, dest_slot),
+                (patches_hbm.at[0], patches),
+                (w_hbm, w_all),
+                (grad_hbm.at[0], out_grad),
+            )
+        )
+    ]
+    for load in loads:
+        load.start()
+
     barrier = pltpu.get_barrier_semaphore()
 
     @pl.loop(1, NSEQ)
@@ -167,16 +197,15 @@
             barrier, inc=1, device_id={"clip": (j + k) % n_clip}, device_id_type=MESH
         )
 
-    w_copy = pltpu.make_async_copy(w_hbm, w_all, w_sem)
-    w_copy.start()
-
+    for load in loads[0:4]:
+        load.wait()
     seg = segment[...]
     tgt = dest_shard[...]
     slot = dest_slot[...]
     hit = iota((192, 196), 0) == seg
     member = onehot(hit)
     counts = jnp.sum(jnp.where(hit, 1.0, 0.0), axis=1, keepdims=True)
-    sums = mm(member, patches[0])
+    sums = mm(member, patches[...])
     tokens = (sums * (1.0 / jnp.maximum(counts, 1.0))).astype(BF)
     to_shard = iota((NSEQ, 192), 0) == tgt
     shard_hot = onehot(to_shard)
@@ -185,20 +214,22 @@
     rank = jnp.sum(jnp.where(to_shard, before, 0.0), axis=0, keepdims=True)
     position = jnp.where(tgt >= 0, tgt.astype(F32) * CAP + rank, -1.0)
     chooser = onehot(iota((NMSG, 192), 0).astype(F32) == position)
-    slot_rows = jnp.where(
-        iota((128, 192), 0).astype(F32) == rank, slot.astype(F32) + 1.0, 0.0
-    ).astype(BF)
-    slot_table = mm_nt(shard_hot, slot_rows).astype(BF)
-    spread = onehot(iota((NMSG, NSEQ), 0) == iota((NMSG, NSEQ), 1) * CAP + 6)
-    slot_cells = mm(spread, slot_table)
-    rows = mm(chooser, tokens)
-    send[:, :, 0:128] = (rows[:, 0:128] + slot_cells).reshape(NSEQ, CAP, 128).astype(BF)
-    send[:, :, 128:] = rows[:, 128:].reshape(NSEQ, CAP, D - 128).astype(BF)
+    same = onehot(iota((192, 192), 0) == iota((192, 192), 1))
+    slot_cells = jnp.broadcast_to(slot.astype(F32) + 1.0, (128, 192)).astype(BF)
+    slot_column = mm_nt(same, slot_cells).astype(BF)
+    rows = mm(chooser, jnp.concatenate([tokens, slot_column], axis=1))
+    send[...] = rows.reshape(NSEQ, CAP, EXT).astype(BF)
 
     pl.semaphore_wait(barrier, NSEQ - 1 + n_clip - 1)
 
     def token_copy(k, peer, lands):
-        return rcopy(send.at[peer], recv.at[lands], a_s.at[k], a_r.at[k], {"seq": peer})
+        return rcopy(
+            send.at[peer, pl.ds(0, TOP)],
+            recv.at[lands, pl.ds(0, TOP)],
+            a_s.at[k],
+            a_r.at[k],
+            {"seq": peer},
+        )
 
     @pl.loop(1, NSEQ)
     def _(k):
@@ -209,42 +240,68 @@
     picker[...] = mm(chooser, member).astype(BF)
     per_patch = mm_tn(member, jnp.broadcast_to(counts, (192, 128)).astype(BF))
     count_inv[...] = 1.0 / per_patch
+    loads[5].wait()
     for blk in range(4):
-        pair = out_grad[0, :, blk * 128 : blk * 128 + 128].astype(F32)
+        pair = out_grad[:, blk * 128 : blk * 128 + 128].astype(F32)
         top, low = pair[0:32], pair[32:64]
-        do_send[2 * blk] = merge_low(top, low).astype(BF)
-        do_send[2 * blk + 1] = merge_high(top, low).astype(BF)
-    w_copy.wait()
-    lane0 = pl.multiple_of(y * 128, 128)
-    w_q = w_all[:, pl.ds(lane0, 128)].astype(F32)
-    w_k = w_all[:, pl.ds(pl.multiple_of(lane0 + 512, 128), 128)].astype(F32)
-    w_v = w_all[:, pl.ds(pl.multiple_of(lane0 + 1024, 128), 128)].astype(F32)
-    low_half = half_lanes((D, 128))
-    first = c == 0
-    k_low = jnp.where(first, w_k, swap(w_k))
-    v_high = jnp.where(first, swap(w_v), w_v)
-    q_low = jnp.where(first, w_q, swap(w_q))
-    w_head[:, 0:128] = jnp.where(low_half, k_low, v_high).astype(BF)
-    w_head[:, 128:256] = jnp.where(low_half, q_low, 0.0).astype(BF)
+        qd_send[2 * blk, 32:64] = merge_low(top, low).astype(BF)
+        qd_send[2 * blk + 1, 32:64] = merge_high(top, low).astype(BF)
+    loads[4].wait()
 
     @pl.loop(1, NSEQ)
     def _(k):
         src = (i + NSEQ - k) % NSEQ
         token_copy(k, src, src).wait_recv()
 
-    came = recv[...].astype(F32).reshape(NMSG, D).astype(BF)
-    col = iota((NMSG, NMSG), 1)
-    from_row = onehot(iota((NMSG, NMSG), 0) == (col // CAP) * CAP + 6)
-    slot_sq = mm_tn(came[:, 0:128], from_row)[0:8]
-    slot_row = jnp.sum(
-        jnp.where(iota((8, NMSG), 0) == iota((8, NMSG), 1) % CAP, slot_sq, 0.0)
-        * jnp.where(iota((8, NMSG), 1) % CAP < 6, 1.0, 0.0),
-        axis=0,
-        keepdims=True,
-    )
+    full = iota((NSEQ, CAP, EXT), 1) < TOP
+    came = jnp.where(full, recv[...].astype(F32), 0.0).reshape(NMSG, EXT).astype(BF)
+    one_lane = onehot(iota((8, 128), 1) == 0)
+    slot_row = mm_nt(one_lane, came[:, D:])[0:1]
     placer = onehot((iota((R, NMSG), 0) + 1).astype(F32) == slot_row)
     placer_ref[...] = placer
-    pq[g] = mm(placer, came).astype(BF)
+    placed = mm(placer, came[:, 0:D]).astype(BF)
+    pq[g] = placed
+
+    def kx_copy(k, peer, lands):
+        return rcopy(
+            kv_send.at[peer],
+            kv.at[x, pl.ds(pl.multiple_of(lands * R, R), R)],
+            kx_s.at[k],
+            kx_r.at[k],
+            {"seq": x * 8 + peer},
+        )
+
+    def qd_copy(k, peer, lands):
+        return rcopy(
+            qd_send.at[peer], qd_recv.at[lands], qd_s.at[k], qd_r.at[k], {"seq": x * 8 + peer}
+        )
+
+    def half_up(v):
+        return v.astype(BF).astype(F32)
+
+    proj = half_up(mm(placed, w_all[:, INNER:]))
+    for blk in range(4):
+        k_blk = proj[:, blk * 128 : blk * 128 + 128]
+        v_blk = proj[:, INNER + blk * 128 : INNER + blk * 128 + 128]
+        kv_send[2 * blk] = merge_low(k_blk, v_blk).astype(BF)
+        kv_send[2 * blk + 1] = merge_high(k_blk, v_blk).astype(BF)
+
+    @pl.loop(1, 8)
+    def _(k):
+        kx_copy(k, (g + k) % 8, g).start()
+
+    kv[x, pl.ds(pl.multiple_of(g * R, R), R)] = kv_send[g]
+    proj_q = half_up(mm(placed, w_all[:, 0:INNER])) * 0.125
+    for blk in range(4):
+        q_blk = proj_q[:, blk * 128 : blk * 128 + 128]
+        qd_send[2 * blk, 0:32] = merge_low(q_blk[0:32], q_blk[32:64]).astype(BF)
+        qd_send[2 * blk + 1, 0:32] = merge_high(q_blk[0:32], q_blk[32:64]).astype(BF)
+
+    @pl.loop(1, 8)
+    def _(k):
+        qd_copy(k, (g + k) % 8, g).start()
+
+    qd_recv[g] = qd_send[g]
 
     g_p, g_m, g_2 = yp * 2 + c, ym * 2 + c, y2 * 2 + c
     A, B = pl.ds(0, 32), pl.ds(32, 32)
@@ -254,37 +311,46 @@
         ref = pq.at[s] if half is None else pq.at[s, half]
         return rcopy(ref, ref, p_s.at[n], p_r.at[n], dev)
 
-    p_copy(0, g, A, to_yp).start()
-    p_copy(1, g, B, to_ym).start()
-    p_copy(2, g, B, to_yp).start()
-    p_copy(3, g, A, to_ym).start()
-    p_copy(4, g, None, to_pal).start()
-    p_copy(0, g_m, A, to_yp).wait_recv()
-    p_copy(5, g_m, A, to_yp).start()
-    p_copy(6, g_m, A, to_pal).start()
-    p_copy(1, g_p, B, to_ym).wait_recv()
-    p_copy(7, g_p, B, to_ym).start()
-    p_copy(8, g_p, B, to_pal).start()
-    p_copy(2, g_m, B, to_yp).wait_recv()
-    p_copy(9, g_m, B, to_pal).start()
-    p_copy(3, g_p, A, to_ym).wait_recv()
-    p_copy(10, g_p, A, to_pal).start()
-    p_copy(5, g_2, A, to_yp).wait_recv()
-    p_copy(11, g_2, A, to_pal).start()
-    p_copy(7, g_2, B, to_ym).wait_recv()
-    p_copy(12, g_2, B, to_pal).start()
     h_p, h_m, h_2, h_g = yp * 2 + 1 - c, ym * 2 + 1 - c, y2 * 2 + 1 - c, y * 2 + 1 - c
-    p_copy(4, h_g, None, to_pal).wait_recv()
-    p_copy(6, h_m, A, to_pal).wait_recv()
-    p_copy(8, h_p, B, to_pal).wait_recv()
-    p_copy(9, h_m, B, to_pal).wait_recv()
-    p_copy(10, h_p, A, to_pal).wait_recv()
-    p_copy(11, h_2, A, to_pal).wait_recv()
-    p_copy(12, h_2, B, to_pal).wait_recv()
-
-    proj = mm(pq[...].reshape(QROWS, D), w_head[...]).astype(BF)
-    kv[x] = proj[:, 0:128]
-    qpad[...] = (proj[:, 128:256].astype(F32) * 0.125).astype(BF)
+
+    def gather_first():
+        p_copy(0, g, A, to_yp).start()
+        p_copy(1, g, B, to_ym).start()
+        p_copy(2, g, B, to_yp).start()
+        p_copy(3, g, A, to_ym).start()
+        p_copy(4, g, None, to_pal).start()
+
+    def gather_second():
+        p_copy(0, g_m, A, to_yp).wait_recv()
+        p_copy(5, g_m, A, to_yp).start()
+        p_copy(6, g_m, A, to_pal).start()
+        p_copy(1, g_p, B, to_ym).wait_recv()
+        p_copy(7, g_p, B, to_ym).start()
+        p_copy(8, g_p, B, to_pal).start()
+        p_copy(2, g_m, B, to_yp).wait_recv()
+        p_copy(9, g_m, B, to_pal).start()
+        p_copy(3, g_p, A, to_ym).wait_recv()
+        p_copy(10, g_p, A, to_pal).start()
+
+    def gather_third():
+        p_copy(5, g_2, A, to_yp).wait_recv()
+        p_copy(11, g_2, A, to_pal).start()
+        p_copy(7, g_2, B, to_ym).wait_recv()
+        p_copy(12, g_2, B, to_pal).start()
+
+    def gather_last():
+        p_copy(4, h_g, None, to_pal).wait_recv()
+        p_copy(6, h_m, A, to_pal).wait_recv()
+        p_copy(8, h_p, B, to_pal).wait_recv()
+        p_copy(9, h_m, B, to_pal).wait_recv()
+        p_copy(10, h_p, A, to_pal).wait_recv()
+        p_copy(11, h_2, A, to_pal).wait_recv()
+        p_copy(12, h_2, B, to_pal).wait_recv()
+
+    @pl.loop(1, 8)
+    def _(k):
+        src = (g + 8 - k) % 8
+        kx_copy(k, src, src).wait_recv()
 
     KA, KB = pl.ds(0, 256), pl.ds(256, 256)
     to_xp, to_xm = seq_dev(xp, y, c), seq_dev(xm, y, c)
@@ -298,16 +364,17 @@
     k_copy(2, x, KB, to_xp).start()
     k_copy(3, x, KA, to_xm).start()
 
-    def do_copy(k, peer, lands):
-        return rcopy(
-            do_send.at[peer], do_recv.at[lands], do_s.at[k], do_r.at[k], {"seq": x * 8 + peer}
-        )
-
-    @pl.loop(1, 8)
-    def _(k):
-        do_copy(k, (g + k) % 8, g).start()
-
-    do_recv[g] = do_send[g]
+    @pl.loop(1, 8)
+    def _(k):
+        src = (g + 8 - k) % 8
+        qd_copy(k, src, src).wait_recv()
+
+    gather_first()
+    qd_in = qd_recv[...].astype(F32)
+    q_in, d_in = qd_in[:, 0:32], qd_in[:, 32:64]
+    low = half_lanes((8, 32, 128))
+    q_rows = jnp.concatenate([jnp.where(low, q_in, 0.0), jnp.where(low, swap(q_in), 0.0)], axis=1)
+    qpad[...] = q_rows.reshape(QROWS, 128).astype(BF)
 
     def forward(s, n):
         kvt[n] = kv[s].astype(F32).T.astype(BF)
@@ -322,6 +389,12 @@
             part_out[n, :, qs] = mm(kvt[n], w.astype(BF))
 
     forward(x, 0)
+    d_rows = jnp.concatenate(
+        [jnp.where(low, 0.0, swap(d_in)), jnp.where(low, 0.0, d_in)], axis=1
+    ).reshape(QROWS, 128)
+    dopad[...] = d_rows.astype(BF)
+    dot_ref[...] = d_rows.T
+
     k_copy(0, xm, KA, to_xp).wait_recv()
     k_copy(4, xm, KA, to_xp).start()
     k_copy(1, xp, KB, to_xm).wait_recv()
@@ -330,19 +403,6 @@
     forward(xm, 1)
     k_copy(3, xp, KA, to_xm).wait_recv()
     forward(xp, 2)
-
-    @pl.loop(1, 8)
-    def _(k):
-        src = (g + 8 - k) % 8
-        do_copy(k, src, src).wait_recv()
-
-    d_in = do_recv[...].astype(F32)
-    high = iota((8, 32, 128), 2) >= 64
-    d_rows = jnp.concatenate(
-        [jnp.where(high, swap(d_in), 0.0), jnp.where(high, d_in, 0.0)], axis=1
-    ).reshape(QROWS, 128)
-    dopad[...] = d_rows.astype(BF)
-    dot_ref[...] = d_rows.T
 
     k_copy(4, x2, KA, to_xp).wait_recv()
     k_copy(5, x2, KB, to_xm).wait_recv()
@@ -372,6 +432,7 @@
 
     att_recv[g] = att_send[g]
 
+    gather_second()
     dq_acc[...] = jnp.zeros((128, QROWS), F32)
 
     def backward(s, n):
@@ -407,6 +468,7 @@
     rs_copy(rs_send2.at[1], rs_recv2.at[1], 3, to_xm).start()
     backward(x, 0)
 
+    gather_third()
     dq_rows = jnp.where(half_lanes((QROWS, 128)), dq_acc[...].T * 0.125, 0.0)
     dq3 = dq_rows.reshape(8, R, 128)
     g_send[:, 64:96] = merge_low(dq3[:, 0:32], dq3[:, 32:64]).astype(BF)
@@ -426,6 +488,7 @@
 
     g_recv[g] = g_send[g]
 
+    gather_last()
     grads = jnp.concatenate([dkv, dq_rows.astype(BF)], axis=1)
     w_part = mm_tn(grads, pq[...].reshape(QROWS, D))
     for q in range(4):
@@ -444,12 +507,28 @@
         src = (g + 8 - k) % 8
         at_copy(k, src, src).wait_recv()
 
+    stores = [
+        pltpu.make_async_copy(a, b, out_sem.at[n])
+        for n, (a, b) in enumerate(
+            ((att_out, att_hbm.at[0]), (patch_out, patch_hbm.at[0]), (weight_out, weight_hbm))
+        )
+    ]
     for blk in range(4):
         a0 = att_recv[2 * blk].astype(F32)
         a1 = att_recv[2 * blk + 1].astype(F32)
         lanes = slice(blk * 128, blk * 128 + 128)
-        att_out[0, 0:32, lanes] = merge_low(a0, a1).astype(BF)
-        att_out[0, 32:64, lanes] = merge_high(a0, a1).astype(BF)
+        att_out[0:32, lanes] = merge_low(a0, a1).astype(BF)
+        att_out[32:64, lanes] = merge_high(a0, a1).astype(BF)
+    stores[0].start()
+
+    ws_copy(ws_send.at[0], ws_recv.at[0], 0, to_xp).wait_recv()
+    ws_send2[0, 0:96] = (wblk[xp, 0:96] + ws_recv[0].astype(F32)).astype(BF)
+    ws_send2[0, 96:192] = wblk[xp, 96:192].astype(BF)
+    ws_copy(ws_send2.at[0], ws_recv2.at[0], 2, to_xp).start()
+    ws_copy(ws_send.at[1], ws_recv.at[1], 1, to_xm).wait_recv()
+    ws_send2[1, 0:96] = wblk[xm, 0:96].astype(BF)
+    ws_send2[1, 96:192] = (wblk[xm, 96:192] + ws_recv[1].astype(F32)).astype(BF)
+    ws_copy(ws_send2.at[1], ws_recv2.at[1], 3, to_xm).start()
 
     @pl.loop(1, 8)
     def _(k):
@@ -464,29 +543,28 @@
         gnat[32:64, q_at : q_at + 128] = merge_high(r0[64:96], r1[64:96]).astype(BF)
         gnat[:, k_at : k_at + 128] = merge_low(r0[0:64], r1[0:64]).astype(BF)
         gnat[:, v_at : v_at + 128] = merge_high(r0[0:64], r1[0:64]).astype(BF)
-    placed_grad = mm_nt(gnat[...], w_all[...]).astype(BF)
-    back = mm_tn(placer_ref[...], placed_grad)
-    back_send[...] = back.reshape(NSEQ, CAP, D).astype(BF)
-
-    def back_copy(k, peer, lands):
+    def back_copy(h, k, peer, lands):
         return rcopy(
-            back_send.at[peer], back_recv.at[lands], b_s.at[k], b_r.at[k], {"seq": peer}
-        )
-
-    @pl.loop(1, NSEQ)
-    def _(k):
-        back_copy(k, (i + k) % NSEQ, i).start()
-
-    back_recv[i] = back_send[i]
-
-    ws_copy(ws_send.at[0], ws_recv.at[0], 0, to_xp).wait_recv()
-    ws_send2[0, 0:96] = (wblk[xp, 0:96] + ws_recv[0].astype(F32)).astype(BF)
-    ws_send2[0, 96:192] = wblk[xp, 96:192].astype(BF)
-    ws_copy(ws_send2.at[0], ws_recv2.at[0], 2, to_xp).start()
-    ws_copy(ws_send.at[1], ws_recv.at[1], 1, to_xm).wait_recv()
-    ws_send2[1, 0:96] = wblk[xm, 0:96].astype(BF)
-    ws_send2[1, 96:192] = (wblk[xm, 96:192] + ws_recv[1].astype(F32)).astype(BF)
-    ws_copy(ws_send2.at[1], ws_recv2.at[1], 3, to_xm).start()
+            back_send.at[h, peer, pl.ds(0, TOP)],
+            back_recv.at[h, lands, pl.ds(0, TOP)],
+            b_s.at[h, k],
+            b_r.at[h, k],
+            {"seq": peer},
+        )
+
+    def send_back(h):
+        grad = mm_nt(gnat[...], w_all[h * HALF : h * HALF + HALF, :]).astype(BF)
+        back = mm_tn(placer_ref[...], grad)
+        back_send[h] = back.reshape(NSEQ, CAP, HALF).astype(BF)
+
+        @pl.loop(1, NSEQ)
+        def _(k):
+            back_copy(h, k, (i + k) % NSEQ, i).start()
+
+        back_recv[h, i] = back_send[h, i]
+
+    send_back(0)
+
     ws_copy(ws_send2.at[0], ws_recv2.at[0], 2, to_xp).wait_recv()
     ws_copy(ws_send2.at[1], ws_recv2.at[1], 3, to_xm).wait_recv()
     w_sum = wblk[x] + ws_recv2[0].astype(F32) + ws_recv2[1].astype(F32)
@@ -510,6 +588,8 @@
         w15_copy(k, (g + k) % 8, g).start()
 
     w15_recv[g] = w15_send[g]
+
+    send_back(1)
 
     @pl.loop(1, 8)
     def _(k):
@@ -553,14 +633,19 @@
 
     w2_recv[j] = w2_send[j]
 
-    @pl.loop(1, NSEQ)
-    def _(k):
-        src = (i + NSEQ - k) % NSEQ
-        back_copy(k, src, src).wait_recv()
-
-    returned = back_recv[...].astype(F32).reshape(NMSG, D).astype(BF)
-    patch_rows = mm_tn(picker[...], returned)
-    patch_out[0] = (patch_rows * count_inv[:, 0:1]).astype(BF)
+    some = iota((NSEQ, CAP, HALF), 1) < TOP
+    for h in range(2):
+
+        @pl.loop(1, NSEQ)
+        def _(k):
+            src = (i + NSEQ - k) % NSEQ
+            back_copy(h, k, src, src).wait_recv()
+
+        returned = jnp.where(some, back_recv[h].astype(F32), 0.0).reshape(NMSG, HALF)
+        patch_rows = mm_tn(picker[...], returned.astype(BF))
+        patch_out[:, h * HALF : h * HALF + HALF] = (patch_rows * count_inv[:, 0:1]).astype(BF)
+
+    stores[1].start()
 
     @pl.loop(1, n_clip)
     def _(k):
@@ -568,16 +653,19 @@
         w2_copy(k, src, src).wait_recv()
 
     weight_out[...] = jnp.sum(w2_recv[...].astype(F32), axis=0)[:, 0:width]
+    stores[2].start()
 
     @pl.loop(1, NSEQ)
     def _(k):
         token_copy(k, (i + k) % NSEQ, i).wait_send()
-        back_copy(k, (i + k) % NSEQ, i).wait_send()
+        back_copy(0, k, (i + k) % NSEQ, i).wait_send()
+        back_copy(1, k, (i + k) % NSEQ, i).wait_send()
 
     @pl.loop(1, 8)
     def _(k):
         peer = (g + k) % 8
-        do_copy(k, peer, g).wait_send()
+        kx_copy(k, peer, g).wait_send()
+        qd_copy(k, peer, g).wait_send()
         at_copy(k, peer, g).wait_send()
         g_copy(k, peer, g).wait_send()
         w15_copy(k, peer, g).wait_send()
@@ -616,20 +704,42 @@
         rs_copy(rs_send2.at[n], rs_recv2.at[n], n + 2, dev).wait_send()
         ws_copy(ws_send.at[n], ws_recv.at[n], n, dev).wait_send()
         ws_copy(ws_send2.at[n], ws_recv2.at[n], n + 2, dev).wait_send()
+    for store in stores:
+        store.wait()
+
+
+def hand_over(att, patch, weight, att_out, patch_out, weight_out, *scratch):
+    bufs, sems = scratch[0:3], scratch[3]
+    trios = tuple(zip((att, patch, weight), bufs, (att_out, patch_out, weight_out)))
+    come = [pltpu.make_async_copy(a, b, sems.at[n]) for n, (a, b, _) in enumerate(trios)]
+    leave = [pltpu.make_async_copy(b, o, sems.at[3 + n]) for n, (_, b, o) in enumerate(trios)]
+    for move in come:
+        move.start()
+    for n in range(3):
+        come[n].wait()
+        leave[n].start()
+    for move in leave:
+        move.wait()
 
 
 def local(patches, segment, dest_shard, dest_slot, w_qkv, out_grad):
     n_clip = lax.axis_size("clip")
     v = pltpu.VMEM
     dma = pltpu.SemaphoreType.DMA
-    vmem = pl.BlockSpec(memory_space=pltpu.VMEM)
     scratch = [
-        v((NSEQ, CAP, D), BF),
-        v((NSEQ, CAP, D), BF),
-        v((NSEQ, CAP, D), BF),
-        v((NSEQ, CAP, D), BF),
+        v((196, D), BF),
+        v((1, 196), I32),
+        v((1, 192), I32),
+        v((1, 192), I32),
+        v((R, INNER), BF),
+        v((R, INNER), BF),
+        v((196, D), BF),
+        v((32, 3 * INNER // n_clip), F32),
+        v((NSEQ, CAP, EXT), BF),
+        v((NSEQ, CAP, EXT), BF),
+        v((2, NSEQ, CAP, HALF), BF),
+        v((2, NSEQ, CAP, HALF), BF),
         v((D, 3 * INNER), BF),
-        v((D, 256), BF),
         v((NMSG, 196), BF),
         v((R, NMSG), BF),
         v((196, 128), F32),
@@ -639,8 +749,9 @@
         v((QROWS, 128), BF),
         v((QROWS, 128), BF),
         v((128, QROWS), F32),
-        v((8, 32, 128), BF),
-        v((8, 32, 128), BF),
+        v((8, R, 128), BF),
+        v((8, R, 128), BF),
+        v((8, R, 128), BF),
         v((4, QROWS, QROWS), F32),
         v((4, 128, QROWS), F32),
         v((4, 1, QROWS), F32),
@@ -667,11 +778,12 @@
         v((8, 48, 128), BF),
         v((n_clip, 32, 128), BF),
         v((n_clip, 32, 128), BF),
-        dma,
+        dma((6,)),
+        dma((3,)),
         dma((NSEQ,)),
         dma((NSEQ,)),
-        dma((NSEQ,)),
-        dma((NSEQ,)),
+        dma((2, NSEQ)),
+        dma((2, NSEQ)),
         dma((13,)),
         dma((13,)),
         dma((6,)),
@@ -680,6 +792,8 @@
         dma((8,)),
         dma((8,)),
         dma((8,)),
+        dma((8,)),
+        dma((8,)),
         dma((4,)),
         dma((4,)),
         dma((8,)),
@@ -691,21 +805,31 @@
         dma((n_clip,)),
         dma((n_clip,)),
     ]
-    return pl.pallas_call(
+    anywhere = pl.BlockSpec(memory_space=pl.ANY)
+    shapes = (
+        jax.ShapeDtypeStruct((1, R, INNER), BF),
+        jax.ShapeDtypeStruct((1, 196, D), BF),
+        jax.ShapeDtypeStruct((32, 3 * INNER // n_clip), F32),
+    )
+    results = pl.pallas_call(
         functools.partial(kernel, n_clip),
-        out_shape=(
-            jax.ShapeDtypeStruct((1, R, INNER), BF),
-            jax.ShapeDtypeStruct((1, 196, D), BF),
-            jax.ShapeDtypeStruct((32, 3 * INNER // n_clip), F32),
-        ),
-        in_specs=[vmem, vmem, vmem, vmem, pl.BlockSpec(memory_space=pl.ANY), vmem],
-        out_specs=(vmem, vmem, vmem),
+        out_shape=shapes,
+        in_specs=[anywhere] * 6,
+        out_specs=(anywhere,) * 3,
         scratch_shapes=scratch,
         compiler_params=pltpu.CompilerParams(
-            collective_id=0, has_side_effects=True, vmem_limit_bytes=56 * 1024 * 1024
+            collective_id=0, has_side_effects=True, vmem_limit_bytes=67_043_328
         ),
         name="rebalance_attention",
     )(patches, segment, dest_shard, dest_slot, w_qkv, out_grad)
+    return pl.pallas_call(
+        hand_over,
+        out_shape=shapes,
+        in_specs=[anywhere] * 3,
+        out_specs=(anywhere,) * 3,
+        scratch_shapes=[v(t.shape, t.dtype) for t in shapes] + [dma((6,))],
+        name="hand_over",
+    )(*results)
 
 
 def solution(mesh):

time: 104 us -> 86.6 us (0.83)
  Pallas kernels: 98.4 us -> 85.8 us
  local copies, waits for them, and re-layouts: 4.57 us -> 0 us
    pallas_call x1 -> x2, Pallas kernels: 98.4 us -> 85.8 us  [the longest x1 83.9 us: local(): pl.pallas_call(functools.partial(kernel, n_clip), out_shape=shapes, in_sp...]
    unnamed x3 -> x0, local copies, waits for them, and re-layouts: 4.57 us -> none
where the time goes in v2:
time: 86.6 us; the launch traced here: 86.4 us
  Pallas kernels  85.8 us (99%)
    pallas_call x1, Pallas kernels, local(): pl.pallas_call(functools.partial(kernel, n_clip), out_shape=shapes, in_sp...  83.9 us
    pallas_call x1, Pallas kernels, local(): pl.pallas_call(hand_over, out_shape=shapes, in_specs=[anywhere] * 3, out_...  1.85 us

profile of v2, /device:TPU:1, one launch (start us, length us, event | category | flops | bytes accessed | tf_op | source)
XLA Modules:
  0.0 86.4 jit_solution(7696337092378307391)
XLA Ops:
  0.6 83.9 %rebalance_attention.1 = (bf16[1,64,512]{2,1,0:T(8,128)(2,1)}, bf16[1,196,1024]{2,1,0:T(8,128)(2,1)}, f32[32,96]{1,0:T(8,128)}) custom-call(bf16[1,196,1024]{2,1,0:T(8,128)(2,1)} %patches_hbm.1, s32[1,196]{1,0:T(1,128)} %segment_hbm.1, s32[1,192]{1,0:T(1,128)} %shard_hbm.1, s32[1,192]{1,0:T(1,128)} %slot_hbm.1, bf16[1024,1536]{1,0:T(8,128)(2,1)} %w_hbm.1, ...), custom_call_target="tpu_custom_call" | custom-call | tf_op jit(solution)/shard_map/rebalance_attention/pallas_call | solution.py:814
  84.6 1.8 %hand_over.1 = (bf16[1,64,512]{2,1,0:T(8,128)(2,1)}, bf16[1,196,1024]{2,1,0:T(8,128)(2,1)}, f32[32,96]{1,0:T(8,128)}) custom-call(bf16[1,64,512]{2,1,0:T(8,128)(2,1)} %get-tuple-element.6.att, bf16[1,196,1024]{2,1,0:T(8,128)(2,1)} %get-tuple-element.7.patch, f32[32,96]{1,0:T(8,128)} %get-tuple-element.8.weight), custom_call_target="tpu_custom_call" | custom-call | tf_op jit(solution)/shard_map/hand_over/pallas_call | solution.py:825

commit v3 on v2

--- a/solution.py
+++ b/solution.py
@@ -95,8 +95,10 @@
     dopad,
     dot_ref,
     kv_send,
-    qd_send,
-    qd_recv,
+    q_send,
+    q_recv,
+    do_send,
+    do_recv,
     weights,
     part_out,
     stat_max,
@@ -109,16 +111,12 @@
     dq_acc,
     rs_send,
     rs_recv,
-    rs_send2,
-    rs_recv2,
     g_send,
     g_recv,
     gnat,
     wblk,
     ws_send,
     ws_recv,
-    ws_send2,
-    ws_recv2,
     w15_send,
     w15_recv,
     w2_send,
@@ -135,8 +133,10 @@
     k_r,
     kx_s,
     kx_r,
-    qd_s,
-    qd_r,
+    q_s,
+    q_r,
+    do_s,
+    do_r,
     at_s,
     at_r,
     rs_s,
@@ -182,6 +182,11 @@
     ]
     for load in loads:
         load.start()
+
+    to_pal = seq_dev(x, y, 1 - c)
+
+    def seven(src, dst, ss, rs):
+        return rcopy(src.at[pl.ds(0, 7)], dst.at[pl.ds(0, 7)], ss, rs, to_pal)
 
     barrier = pltpu.get_barrier_semaphore()
 
@@ -222,18 +227,18 @@
 
     pl.semaphore_wait(barrier, NSEQ - 1 + n_clip - 1)
 
-    def token_copy(k, peer, lands):
+    def token_copy(peer, lands):
         return rcopy(
             send.at[peer, pl.ds(0, TOP)],
             recv.at[lands, pl.ds(0, TOP)],
-            a_s.at[k],
-            a_r.at[k],
+            a_s,
+            a_r,
             {"seq": peer},
         )
 
     @pl.loop(1, NSEQ)
     def _(k):
-        token_copy(k, (i + k) % NSEQ, i).start()
+        token_copy((i + k) % NSEQ, i).start()
 
     recv[i] = send[i]
 
@@ -244,14 +249,15 @@
     for blk in range(4):
         pair = out_grad[:, blk * 128 : blk * 128 + 128].astype(F32)
         top, low = pair[0:32], pair[32:64]
-        qd_send[2 * blk, 32:64] = merge_low(top, low).astype(BF)
-        qd_send[2 * blk + 1, 32:64] = merge_high(top, low).astype(BF)
+        do_send[2 * blk] = merge_low(top, low).astype(BF)
+        do_send[2 * blk + 1] = merge_high(top, low).astype(BF)
     loads[4].wait()
 
-    @pl.loop(1, NSEQ)
-    def _(k):
-        src = (i + NSEQ - k) % NSEQ
-        token_copy(k, src, src).wait_recv()
+    def token_all():
+        part = (pl.ds(0, NSEQ - 1), pl.ds(0, TOP))
+        return rcopy(send.at[part], recv.at[part], a_s, a_r, to_pal)
+
+    token_all().wait_recv()
 
     full = iota((NSEQ, CAP, EXT), 1) < TOP
     came = jnp.where(full, recv[...].astype(F32), 0.0).reshape(NMSG, EXT).astype(BF)
@@ -262,19 +268,20 @@
     placed = mm(placer, came[:, 0:D]).astype(BF)
     pq[g] = placed
 
-    def kx_copy(k, peer, lands):
+    def kx_copy(peer, lands):
         return rcopy(
             kv_send.at[peer],
             kv.at[x, pl.ds(pl.multiple_of(lands * R, R), R)],
-            kx_s.at[k],
-            kx_r.at[k],
+            kx_s,
+            kx_r,
             {"seq": x * 8 + peer},
         )
 
-    def qd_copy(k, peer, lands):
-        return rcopy(
-            qd_send.at[peer], qd_recv.at[lands], qd_s.at[k], qd_r.at[k], {"seq": x * 8 + peer}
-        )
+    def q_copy(peer, lands):
+        return rcopy(q_send.at[peer], q_recv.at[lands], q_s, q_r, {"seq": x * 8 + peer})
+
+    def do_copy(peer, lands):
+        return rcopy(do_send.at[peer], do_recv.at[lands], do_s, do_r, {"seq": x * 8 + peer})
 
     def half_up(v):
         return v.astype(BF).astype(F32)
@@ -288,28 +295,33 @@
 
     @pl.loop(1, 8)
     def _(k):
-        kx_copy(k, (g + k) % 8, g).start()
+        kx_copy((g + k) % 8, g).start()
 
     kv[x, pl.ds(pl.multiple_of(g * R, R), R)] = kv_send[g]
     proj_q = half_up(mm(placed, w_all[:, 0:INNER])) * 0.125
     for blk in range(4):
         q_blk = proj_q[:, blk * 128 : blk * 128 + 128]
-        qd_send[2 * blk, 0:32] = merge_low(q_blk[0:32], q_blk[32:64]).astype(BF)
-        qd_send[2 * blk + 1, 0:32] = merge_high(q_blk[0:32], q_blk[32:64]).astype(BF)
+        q_send[2 * blk] = merge_low(q_blk[0:32], q_blk[32:64]).astype(BF)
+        q_send[2 * blk + 1] = merge_high(q_blk[0:32], q_blk[32:64]).astype(BF)
 
     @pl.loop(1, 8)
     def _(k):
-        qd_copy(k, (g + k) % 8, g).start()
-
-    qd_recv[g] = qd_send[g]
+        q_copy((g + k) % 8, g).start()
+
+    @pl.loop(1, 8)
+    def _(k):
+        do_copy((g + k) % 8, g).start()
+
+    q_recv[g] = q_send[g]
+    do_recv[g] = do_send[g]
 
     g_p, g_m, g_2 = yp * 2 + c, ym * 2 + c, y2 * 2 + c
     A, B = pl.ds(0, 32), pl.ds(32, 32)
-    to_yp, to_ym, to_pal = seq_dev(x, yp, c), seq_dev(x, ym, c), seq_dev(x, y, 1 - c)
+    to_yp, to_ym = seq_dev(x, yp, c), seq_dev(x, ym, c)
 
     def p_copy(n, s, half, dev):
         ref = pq.at[s] if half is None else pq.at[s, half]
-        return rcopy(ref, ref, p_s.at[n], p_r.at[n], dev)
+        return rcopy(ref, ref, p_s, p_r.at[n], dev)
 
     h_p, h_m, h_2, h_g = yp * 2 + 1 - c, ym * 2 + 1 - c, y2 * 2 + 1 - c, y * 2 + 1 - c
 
@@ -347,31 +359,26 @@
         p_copy(11, h_2, A, to_pal).wait_recv()
         p_copy(12, h_2, B, to_pal).wait_recv()
 
-    @pl.loop(1, 8)
-    def _(k):
-        src = (g + 8 - k) % 8
-        kx_copy(k, src, src).wait_recv()
-
+    def kx_all():
+        part = pl.ds(0, 7 * R)
+        return rcopy(kv.at[x, part], kv.at[x, part], kx_s, kx_r, to_pal)
+
+    kx_all().wait_recv()
     KA, KB = pl.ds(0, 256), pl.ds(256, 256)
     to_xp, to_xm = seq_dev(xp, y, c), seq_dev(xm, y, c)
 
     def k_copy(n, s, half, dev):
         ref = kv.at[s, half]
-        return rcopy(ref, ref, k_s.at[n], k_r.at[n], dev)
+        return rcopy(ref, ref, k_s, k_r.at[n], dev)
 
     k_copy(0, x, KA, to_xp).start()
     k_copy(1, x, KB, to_xm).start()
     k_copy(2, x, KB, to_xp).start()
     k_copy(3, x, KA, to_xm).start()
 
-    @pl.loop(1, 8)
-    def _(k):
-        src = (g + 8 - k) % 8
-        qd_copy(k, src, src).wait_recv()
-
+    seven(q_send, q_recv, q_s, q_r).wait_recv()
     gather_first()
-    qd_in = qd_recv[...].astype(F32)
-    q_in, d_in = qd_in[:, 0:32], qd_in[:, 32:64]
+    q_in = q_recv[...].astype(F32)
     low = half_lanes((8, 32, 128))
     q_rows = jnp.concatenate([jnp.where(low, q_in, 0.0), jnp.where(low, swap(q_in), 0.0)], axis=1)
     qpad[...] = q_rows.reshape(QROWS, 128).astype(BF)
@@ -389,6 +396,8 @@
             part_out[n, :, qs] = mm(kvt[n], w.astype(BF))
 
     forward(x, 0)
+    seven(do_send, do_recv, do_s, do_r).wait_recv()
+    d_in = do_recv[...].astype(F32)
     d_rows = jnp.concatenate(
         [jnp.where(low, 0.0, swap(d_in)), jnp.where(low, 0.0, d_in)], axis=1
     ).reshape(QROWS, 128)
@@ -421,14 +430,12 @@
     att3 = att_half.T.reshape(8, R, 128)
     att_send[...] = merge_high(att3[:, 0:32], att3[:, 32:64]).astype(BF)
 
-    def at_copy(k, peer, lands):
-        return rcopy(
-            att_send.at[peer], att_recv.at[lands], at_s.at[k], at_r.at[k], {"seq": x * 8 + peer}
-        )
+    def at_copy(peer, lands):
+        return rcopy(att_send.at[peer], att_recv.at[lands], at_s, at_r, {"seq": x * 8 + peer})
 
     @pl.loop(1, 8)
     def _(k):
-        at_copy(k, (g + k) % 8, g).start()
+        at_copy((g + k) % 8, g).start()
 
     att_recv[g] = att_send[g]
 
@@ -443,48 +450,71 @@
             score_grad = (prob * (prob_grad - gd_ref[:, qs])).astype(BF)
             upd = mm(score_grad, qpad[qs, :]) + mm(prob.astype(BF), dopad[qs, :])
             if q == 0:
-                dkv_acc[...] = upd
+                dkv_acc[n] = upd
             else:
-                dkv_acc[...] += upd
+                dkv_acc[n] += upd
             dq_acc[:, qs] += mm(kvt[n], score_grad)
 
-    def rs_copy(src, dst, n, dev):
-        return rcopy(src, dst, rs_s.at[n], rs_r.at[n], dev)
-
+    def ring_sum(sends, recvs, ss, rs, part, rows):
+        half = rows // 2
+
+        def copy(n, dev):
+            return rcopy(sends.at[n], recvs.at[n], ss, rs.at[n], dev)
+
+        def put(n, value, dev):
+            sends[n] = value.astype(BF)
+            copy(n, dev).start()
+
+        def first():
+            put(0, part(x2, 3, slice(0, half)), to_xp)
+            put(1, part(x2, 3, slice(half, rows)), to_xm)
+
+        def second():
+            put(2, part(xp, 2, slice(half, rows)), to_xp)
+
+        def third():
+            put(3, part(xm, 1, slice(0, half)), to_xm)
+
+        def fourth():
+            copy(0, to_xp).wait_recv()
+            put(4, part(xp, 2, slice(0, half)) + recvs[0].astype(F32), to_xp)
+            copy(1, to_xm).wait_recv()
+            put(5, part(xm, 1, slice(half, rows)) + recvs[1].astype(F32), to_xm)
+
+        def fifth():
+            for n, dev in ((2, to_xp), (3, to_xm), (4, to_xp), (5, to_xm)):
+                copy(n, dev).wait_recv()
+            up = recvs[4].astype(F32) + recvs[3].astype(F32)
+            down = recvs[2].astype(F32) + recvs[5].astype(F32)
+            return part(x, 0, slice(0, rows)) + jnp.concatenate([up, down], axis=0)
+
+        def sent():
+            rcopy(sends, recvs, ss, rs.at[0], to_xp).wait_send()
+
+        return first, second, third, fourth, fifth, sent
+
+    rs = ring_sum(rs_send, rs_recv, rs_s, rs_r, lambda s, n, part: dkv_acc[n, part], QROWS)
     backward(x2, 3)
-    rs_send[0] = dkv_acc[0:256].astype(BF)
-    rs_send[1] = dkv_acc[256:512].astype(BF)
-    rs_copy(rs_send.at[0], rs_recv.at[0], 0, to_xp).start()
-    rs_copy(rs_send.at[1], rs_recv.at[1], 1, to_xm).start()
+    rs[0]()
     backward(xp, 2)
-    rs_copy(rs_send.at[0], rs_recv.at[0], 0, to_xp).wait_recv()
-    rs_send2[0, 0:256] = (dkv_acc[0:256] + rs_recv[0].astype(F32)).astype(BF)
-    rs_send2[0, 256:512] = dkv_acc[256:512].astype(BF)
-    rs_copy(rs_send2.at[0], rs_recv2.at[0], 2, to_xp).start()
+    rs[1]()
     backward(xm, 1)
-    rs_copy(rs_send.at[1], rs_recv.at[1], 1, to_xm).wait_recv()
-    rs_send2[1, 0:256] = dkv_acc[0:256].astype(BF)
-    rs_send2[1, 256:512] = (dkv_acc[256:512] + rs_recv[1].astype(F32)).astype(BF)
-    rs_copy(rs_send2.at[1], rs_recv2.at[1], 3, to_xm).start()
+    rs[2]()
     backward(x, 0)
-
+    rs[3]()
     gather_third()
     dq_rows = jnp.where(half_lanes((QROWS, 128)), dq_acc[...].T * 0.125, 0.0)
     dq3 = dq_rows.reshape(8, R, 128)
     g_send[:, 64:96] = merge_low(dq3[:, 0:32], dq3[:, 32:64]).astype(BF)
-    rs_copy(rs_send2.at[0], rs_recv2.at[0], 2, to_xp).wait_recv()
-    rs_copy(rs_send2.at[1], rs_recv2.at[1], 3, to_xm).wait_recv()
-    dkv = (dkv_acc[...] + rs_recv2[0].astype(F32) + rs_recv2[1].astype(F32)).astype(BF)
+    dkv = rs[4]().astype(BF)
     g_send[:, 0:64] = dkv.reshape(8, R, 128)
 
-    def g_copy(k, peer, lands):
-        return rcopy(
-            g_send.at[peer], g_recv.at[lands], g_s.at[k], g_r.at[k], {"seq": x * 8 + peer}
-        )
+    def g_copy(peer, lands):
+        return rcopy(g_send.at[peer], g_recv.at[lands], g_s, g_r, {"seq": x * 8 + peer})
 
     @pl.loop(1, 8)
     def _(k):
-        g_copy(k, (g + k) % 8, g).start()
+        g_copy((g + k) % 8, g).start()
 
     g_recv[g] = g_send[g]
 
@@ -494,19 +524,11 @@
     for q in range(4):
         wblk[q] = w_part[0:192, q * 256 : q * 256 + 256]
 
-    def ws_copy(src, dst, n, dev):
-        return rcopy(src, dst, ws_s.at[n], ws_r.at[n], dev)
-
-    ws_send[0] = wblk[x2, 0:96].astype(BF)
-    ws_send[1] = wblk[x2, 96:192].astype(BF)
-    ws_copy(ws_send.at[0], ws_recv.at[0], 0, to_xp).start()
-    ws_copy(ws_send.at[1], ws_recv.at[1], 1, to_xm).start()
-
-    @pl.loop(1, 8)
-    def _(k):
-        src = (g + 8 - k) % 8
-        at_copy(k, src, src).wait_recv()
-
+    ws = ring_sum(ws_send, ws_recv, ws_s, ws_r, lambda s, n, part: wblk[s, part], 192)
+    for step in ws[0:3]:
+        step()
+
+    seven(att_send, att_recv, at_s, at_r).wait_recv()
     stores = [
         pltpu.make_async_copy(a, b, out_sem.at[n])
         for n, (a, b) in enumerate(
@@ -521,20 +543,9 @@
         att_out[32:64, lanes] = merge_high(a0, a1).astype(BF)
     stores[0].start()
 
-    ws_copy(ws_send.at[0], ws_recv.at[0], 0, to_xp).wait_recv()
-    ws_send2[0, 0:96] = (wblk[xp, 0:96] + ws_recv[0].astype(F32)).astype(BF)
-    ws_send2[0, 96:192] = wblk[xp, 96:192].astype(BF)
-    ws_copy(ws_send2.at[0], ws_recv2.at[0], 2, to_xp).start()
-    ws_copy(ws_send.at[1], ws_recv.at[1], 1, to_xm).wait_recv()
-    ws_send2[1, 0:96] = wblk[xm, 0:96].astype(BF)
-    ws_send2[1, 96:192] = (wblk[xm, 96:192] + ws_recv[1].astype(F32)).astype(BF)
-    ws_copy(ws_send2.at[1], ws_recv2.at[1], 3, to_xm).start()
-
-    @pl.loop(1, 8)
-    def _(k):
-        src = (g + 8 - k) % 8
-        g_copy(k, src, src).wait_recv()
-
+    ws[3]()
+
+    seven(g_send, g_recv, g_s, g_r).wait_recv()
     for blk in range(4):
         r0 = g_recv[2 * blk].astype(F32)
         r1 = g_recv[2 * blk + 1].astype(F32)
@@ -543,12 +554,12 @@
         gnat[32:64, q_at : q_at + 128] = merge_high(r0[64:96], r1[64:96]).astype(BF)
         gnat[:, k_at : k_at + 128] = merge_low(r0[0:64], r1[0:64]).astype(BF)
         gnat[:, v_at : v_at + 128] = merge_high(r0[0:64], r1[0:64]).astype(BF)
-    def back_copy(h, k, peer, lands):
+    def back_copy(h, peer, lands):
         return rcopy(
             back_send.at[h, peer, pl.ds(0, TOP)],
             back_recv.at[h, lands, pl.ds(0, TOP)],
-            b_s.at[h, k],
-            b_r.at[h, k],
+            b_s,
+            b_r.at[h],
             {"seq": peer},
         )
 
@@ -559,43 +570,32 @@
 
         @pl.loop(1, NSEQ)
         def _(k):
-            back_copy(h, k, (i + k) % NSEQ, i).start()
+            back_copy(h, (i + k) % NSEQ, i).start()
 
         back_recv[h, i] = back_send[h, i]
 
-    send_back(0)
-
-    ws_copy(ws_send2.at[0], ws_recv2.at[0], 2, to_xp).wait_recv()
-    ws_copy(ws_send2.at[1], ws_recv2.at[1], 3, to_xm).wait_recv()
-    w_sum = wblk[x] + ws_recv2[0].astype(F32) + ws_recv2[1].astype(F32)
+    w_sum = ws[4]()
     w_kv = w_sum[0:128].T.reshape(8, 32, 128)
     w_qq = jnp.concatenate([w_sum[128:192], jnp.zeros((64, 256), F32)], axis=0)
     w_qq = w_qq.T.reshape(8, 32, 128)
     w15_send[:, 0:32] = w_kv.astype(BF)
     w15_send[:, 32:48] = merge_low(w_qq[:, 0:16], w_qq[:, 16:32]).astype(BF)
 
-    def w15_copy(k, peer, lands):
+    def w15_copy(peer, lands):
         return rcopy(
-            w15_send.at[peer],
-            w15_recv.at[lands],
-            w15_s.at[k],
-            w15_r.at[k],
-            {"seq": x * 8 + peer},
+            w15_send.at[peer], w15_recv.at[lands], w15_s, w15_r, {"seq": x * 8 + peer}
         )
 
     @pl.loop(1, 8)
     def _(k):
-        w15_copy(k, (g + k) % 8, g).start()
+        w15_copy((g + k) % 8, g).start()
 
     w15_recv[g] = w15_send[g]
 
+    send_back(0)
     send_back(1)
 
-    @pl.loop(1, 8)
-    def _(k):
-        src = (g + 8 - k) % 8
-        w15_copy(k, src, src).wait_recv()
-
+    seven(w15_send, w15_recv, w15_s, w15_r).wait_recv()
     q_blocks, k_blocks, v_blocks = [], [], []
     for blk in range(4):
         r0 = w15_recv[2 * blk].astype(F32)
@@ -622,88 +622,47 @@
                 )
         w2_send[n] = piece.astype(BF)
 
-    def w2_copy(k, peer, lands):
-        return rcopy(
-            w2_send.at[peer], w2_recv.at[lands], w2_s.at[k], w2_r.at[k], {"clip": peer}
-        )
+    def w2_copy(peer, lands):
+        return rcopy(w2_send.at[peer], w2_recv.at[lands], w2_s, w2_r, {"clip": peer})
+
+    def w2_all():
+        part = pl.ds(0, n_clip - 1)
+        return rcopy(w2_send.at[part], w2_recv.at[part], w2_s, w2_r, to_pal)
 
     @pl.loop(1, n_clip)
     def _(k):
-        w2_copy(k, (j + k) % n_clip, j).start()
+        w2_copy((j + k) % n_clip, j).start()
 
     w2_recv[j] = w2_send[j]
 
     some = iota((NSEQ, CAP, HALF), 1) < TOP
     for h in range(2):
-
-        @pl.loop(1, NSEQ)
-        def _(k):
-            src = (i + NSEQ - k) % NSEQ
-            back_copy(h, k, src, src).wait_recv()
-
+        part = (pl.ds(0, NSEQ - 1), pl.ds(0, TOP))
+        rcopy(back_send.at[h].at[part], back_recv.at[h].at[part], b_s, b_r.at[h], to_pal).wait_recv()
         returned = jnp.where(some, back_recv[h].astype(F32), 0.0).reshape(NMSG, HALF)
         patch_rows = mm_tn(picker[...], returned.astype(BF))
         patch_out[:, h * HALF : h * HALF + HALF] = (patch_rows * count_inv[:, 0:1]).astype(BF)
 
     stores[1].start()
 
-    @pl.loop(1, n_clip)
-    def _(k):
-        src = (j + n_clip - k) % n_clip
-        w2_copy(k, src, src).wait_recv()
-
+    w2_all().wait_recv()
     weight_out[...] = jnp.sum(w2_recv[...].astype(F32), axis=0)[:, 0:width]
     stores[2].start()
 
-    @pl.loop(1, NSEQ)
-    def _(k):
-        token_copy(k, (i + k) % NSEQ, i).wait_send()
-        back_copy(0, k, (i + k) % NSEQ, i).wait_send()
-        back_copy(1, k, (i + k) % NSEQ, i).wait_send()
-
-    @pl.loop(1, 8)
-    def _(k):
-        peer = (g + k) % 8
-        kx_copy(k, peer, g).wait_send()
-        qd_copy(k, peer, g).wait_send()
-        at_copy(k, peer, g).wait_send()
-        g_copy(k, peer, g).wait_send()
-        w15_copy(k, peer, g).wait_send()
-
-    @pl.loop(1, n_clip)
-    def _(k):
-        w2_copy(k, (j + k) % n_clip, j).wait_send()
-
-    for n, s, half, dev in (
-        (0, g, A, to_yp),
-        (1, g, B, to_ym),
-        (2, g, B, to_yp),
-        (3, g, A, to_ym),
-        (4, g, None, to_pal),
-        (5, g_m, A, to_yp),
-        (6, g_m, A, to_pal),
-        (7, g_p, B, to_ym),
-        (8, g_p, B, to_pal),
-        (9, g_m, B, to_pal),
-        (10, g_p, A, to_pal),
-        (11, g_2, A, to_pal),
-        (12, g_2, B, to_pal),
-    ):
-        p_copy(n, s, half, dev).wait_send()
-    for n, s, half, dev in (
-        (0, x, KA, to_xp),
-        (1, x, KB, to_xm),
-        (2, x, KB, to_xp),
-        (3, x, KA, to_xm),
-        (4, xm, KA, to_xp),
-        (5, xp, KB, to_xm),
-    ):
-        k_copy(n, s, half, dev).wait_send()
-    for n, dev in ((0, to_xp), (1, to_xm)):
-        rs_copy(rs_send.at[n], rs_recv.at[n], n, dev).wait_send()
-        rs_copy(rs_send2.at[n], rs_recv2.at[n], n + 2, dev).wait_send()
-        ws_copy(ws_send.at[n], ws_recv.at[n], n, dev).wait_send()
-        ws_copy(ws_send2.at[n], ws_recv2.at[n], n + 2, dev).wait_send()
+    token_all().wait_send()
+    part = (pl.ds(0, 2), pl.ds(0, NSEQ - 1), pl.ds(0, TOP))
+    rcopy(back_send.at[part], back_recv.at[part], b_s, b_r.at[0], to_pal).wait_send()
+    kx_all().wait_send()
+    seven(q_send, q_recv, q_s, q_r).wait_send()
+    seven(do_send, do_recv, do_s, do_r).wait_send()
+    seven(att_send, att_recv, at_s, at_r).wait_send()
+    seven(g_send, g_recv, g_s, g_r).wait_send()
+    seven(w15_send, w15_recv, w15_s, w15_r).wait_send()
+    w2_all().wait_send()
+    seven(pq, pq, p_s, p_r.at[0]).wait_send()
+    rcopy(kv.at[pl.ds(0, 3)], kv.at[pl.ds(0, 3)], k_s, k_r.at[0], to_xp).wait_send()
+    rs[5]()
+    ws[5]()
     for store in stores:
         store.wait()
 
@@ -750,8 +709,10 @@
         v((QROWS, 128), BF),
         v((128, QROWS), F32),
         v((8, R, 128), BF),
-        v((8, R, 128), BF),
-        v((8, R, 128), BF),
+        v((8, 32, 128), BF),
+        v((8, 32, 128), BF),
+        v((8, 32, 128), BF),
+        v((8, 32, 128), BF),
         v((4, QROWS, QROWS), F32),
         v((4, 128, QROWS), F32),
         v((4, 1, QROWS), F32),
@@ -760,50 +721,48 @@
         v((1, QROWS), F32),
         v((8, 32, 128), BF),
         v((8, 32, 128), BF),
-        v((QROWS, 128), F32),
+        v((4, QROWS, 128), F32),
         v((128, QROWS), F32),
-        v((2, 256, 128), BF),
-        v((2, 256, 128), BF),
-        v((2, QROWS, 128), BF),
-        v((2, QROWS, 128), BF),
+        v((6, 256, 128), BF),
+        v((6, 256, 128), BF),
         v((8, 96, 128), BF),
         v((8, 96, 128), BF),
         v((R, 3 * INNER), BF),
         v((4, 192, 256), F32),
-        v((2, 96, 256), BF),
-        v((2, 96, 256), BF),
-        v((2, 192, 256), BF),
-        v((2, 192, 256), BF),
+        v((6, 96, 256), BF),
+        v((6, 96, 256), BF),
         v((8, 48, 128), BF),
         v((8, 48, 128), BF),
         v((n_clip, 32, 128), BF),
         v((n_clip, 32, 128), BF),
         dma((6,)),
         dma((3,)),
-        dma((NSEQ,)),
-        dma((NSEQ,)),
-        dma((2, NSEQ)),
-        dma((2, NSEQ)),
+        dma,
+        dma,
+        dma,
+        dma((2,)),
+        dma,
         dma((13,)),
-        dma((13,)),
+        dma,
         dma((6,)),
+        dma,
+        dma,
+        dma,
+        dma,
+        dma,
+        dma,
+        dma,
+        dma,
+        dma,
         dma((6,)),
-        dma((8,)),
-        dma((8,)),
-        dma((8,)),
-        dma((8,)),
-        dma((8,)),
-        dma((8,)),
-        dma((4,)),
-        dma((4,)),
-        dma((8,)),
-        dma((8,)),
-        dma((4,)),
-        dma((4,)),
-        dma((8,)),
-        dma((8,)),
-        dma((n_clip,)),
-        dma((n_clip,)),
+        dma,
+        dma,
+        dma,
+        dma((6,)),
+        dma,
+        dma,
+        dma,
+        dma,
     ]
     anywhere = pl.BlockSpec(memory_space=pl.ANY)
     shapes = (

time: 86.6 us -> 79.7 us (0.920)
  Pallas kernels: 85.8 us -> 78.6 us
    pallas_call x1, Pallas kernels: 83.9 us -> 76.8 us  [local(): pl.pallas_call(functools.partial(kernel, n_clip), out_shape=shapes, in_sp...]
where the time goes in v3:
time: 79.7 us; the launch traced here: 79.3 us
  Pallas kernels  78.6 us (99%)
    pallas_call x1, Pallas kernels, local(): pl.pallas_call(functools.partial(kernel, n_clip), out_shape=shapes, in_sp...  76.8 us
    pallas_call x1, Pallas kernels, local(): pl.pallas_call(hand_over, out_shape=shapes, in_specs=[anywhere] * 3, out_...  1.85 us

profile of v3, /device:TPU:1, one launch (start us, length us, event | category | flops | bytes accessed | tf_op | source)
XLA Modules:
  0.0 79.3 jit_solution(6839090314102097011)
XLA Ops:
  0.6 76.8 %rebalance_attention.1 = (bf16[1,64,512]{2,1,0:T(8,128)(2,1)}, bf16[1,196,1024]{2,1,0:T(8,128)(2,1)}, f32[32,96]{1,0:T(8,128)}) custom-call(bf16[1,196,1024]{2,1,0:T(8,128)(2,1)} %patches_hbm.1, s32[1,196]{1,0:T(1,128)} %segment_hbm.1, s32[1,192]{1,0:T(1,128)} %shard_hbm.1, s32[1,192]{1,0:T(1,128)} %slot_hbm.1, bf16[1024,1536]{1,0:T(8,128)(2,1)} %w_hbm.1, ...), custom_call_target="tpu_custom_call" | custom-call | tf_op jit(solution)/shard_map/rebalance_attention/pallas_call | solution.py:773
  77.4 1.8 %hand_over.1 = (bf16[1,64,512]{2,1,0:T(8,128)(2,1)}, bf16[1,196,1024]{2,1,0:T(8,128)(2,1)}, f32[32,96]{1,0:T(8,128)}) custom-call(bf16[1,64,512]{2,1,0:T(8,128)(2,1)} %get-tuple-element.6.att, bf16[1,196,1024]{2,1,0:T(8,128)(2,1)} %get-tuple-element.7.patch, f32[32,96]{1,0:T(8,128)} %get-tuple-element.8.weight), custom_call_target="tpu_custom_call" | custom-call | tf_op jit(solution)/shard_map/hand_over/pallas_call | solution.py:784

commit v4 on v3

--- a/solution.py
+++ b/solution.py
@@ -21,8 +21,7 @@
 QROWS = 512
 QC = 256
 TOP = 6
-EXT = D + 128
-HALF = D // 2
+PARTS = ((0, 512), (512, 384), (896, 128))
 
 
 def iota(shape, dim):
@@ -82,8 +81,12 @@
     weight_out,
     send,
     recv,
-    back_send,
-    back_recv,
+    back_send_0,
+    back_send_1,
+    back_send_2,
+    back_recv_0,
+    back_recv_1,
+    back_recv_2,
     w_all,
     picker,
     placer_ref,
@@ -113,7 +116,10 @@
     rs_recv,
     g_send,
     g_recv,
+    gq_send,
+    gq_recv,
     gnat,
+    pg_acc,
     wblk,
     ws_send,
     ws_recv,
@@ -125,6 +131,8 @@
     out_sem,
     a_s,
     a_r,
+    sl_s,
+    sl_r,
     b_s,
     b_r,
     p_s,
@@ -143,6 +151,8 @@
     rs_r,
     g_s,
     g_r,
+    gq_s,
+    gq_r,
     ws_s,
     ws_r,
     w15_s,
@@ -150,6 +160,8 @@
     w2_s,
     w2_r,
 ):
+    back_send = (back_send_0, back_send_1, back_send_2)
+    back_recv = (back_recv_0, back_recv_1, back_recv_2)
     i = lax.axis_index("seq")
     j = lax.axis_index("clip")
     x = i // 8
@@ -190,19 +202,16 @@
 
     barrier = pltpu.get_barrier_semaphore()
 
-    @pl.loop(1, NSEQ)
-    def _(k):
+    for k in range(1, NSEQ):
         pl.semaphore_signal(
-            barrier, inc=1, device_id={"seq": (i + k) % NSEQ}, device_id_type=MESH
-        )
-
-    @pl.loop(1, n_clip)
-    def _(k):
+            barrier, inc=1, device_id={"seq": lax.rem(i + k, NSEQ)}, device_id_type=MESH
+        )
+    for k in range(1, n_clip):
         pl.semaphore_signal(
-            barrier, inc=1, device_id={"clip": (j + k) % n_clip}, device_id_type=MESH
-        )
-
-    for load in loads[0:4]:
+            barrier, inc=1, device_id={"clip": lax.rem(j + k, n_clip)}, device_id_type=MESH
+        )
+
+    for load in loads[0:3]:
         load.wait()
     seg = segment[...]
     tgt = dest_shard[...]
@@ -210,8 +219,6 @@
     hit = iota((192, 196), 0) == seg
     member = onehot(hit)
     counts = jnp.sum(jnp.where(hit, 1.0, 0.0), axis=1, keepdims=True)
-    sums = mm(member, patches[...])
-    tokens = (sums * (1.0 / jnp.maximum(counts, 1.0))).astype(BF)
     to_shard = iota((NSEQ, 192), 0) == tgt
     shard_hot = onehot(to_shard)
     earlier = onehot(iota((192, 192), 0) < iota((192, 192), 1))
@@ -219,13 +226,30 @@
     rank = jnp.sum(jnp.where(to_shard, before, 0.0), axis=0, keepdims=True)
     position = jnp.where(tgt >= 0, tgt.astype(F32) * CAP + rank, -1.0)
     chooser = onehot(iota((NMSG, 192), 0).astype(F32) == position)
-    same = onehot(iota((192, 192), 0) == iota((192, 192), 1))
-    slot_cells = jnp.broadcast_to(slot.astype(F32) + 1.0, (128, 192)).astype(BF)
-    slot_column = mm_nt(same, slot_cells).astype(BF)
-    rows = mm(chooser, jnp.concatenate([tokens, slot_column], axis=1))
-    send[...] = rows.reshape(NSEQ, CAP, EXT).astype(BF)
+    slot_rows = jnp.where(
+        iota((128, 192), 0).astype(F32) == rank, slot.astype(F32) + 1.0, 0.0
+    ).astype(BF)
+    slot_table = mm_nt(shard_hot, slot_rows).astype(BF)
+    spread = onehot(iota((NMSG, NSEQ), 0) == iota((NMSG, NSEQ), 1) * CAP + TOP)
+    slot_cells = mm(spread, slot_table)
+    loads[3].wait()
+    sums = mm(member, patches[...])
+    tokens = (sums * (1.0 / jnp.maximum(counts, 1.0))).astype(BF)
+    rows = mm(chooser, tokens)
+    send[:, :, 0:128] = (rows[:, 0:128] + slot_cells).reshape(NSEQ, CAP, 128).astype(BF)
+    send[:, :, 128:] = rows[:, 128:].reshape(NSEQ, CAP, D - 128).astype(BF)
 
     pl.semaphore_wait(barrier, NSEQ - 1 + n_clip - 1)
+
+    def slot_copy(peer, lands):
+        part = (pl.ds(TOP, 2), pl.ds(0, 128))
+        return rcopy(
+            send.at[(peer, *part)], recv.at[(lands, *part)], sl_s, sl_r, {"seq": peer}
+        )
+
+    def slot_all():
+        part = (pl.ds(0, NSEQ - 1), pl.ds(TOP, 2), pl.ds(0, 128))
+        return rcopy(send.at[part], recv.at[part], sl_s, sl_r, to_pal)
 
     def token_copy(peer, lands):
         return rcopy(
@@ -238,6 +262,7 @@
 
     @pl.loop(1, NSEQ)
     def _(k):
+        slot_copy((i + k) % NSEQ, i).start()
         token_copy((i + k) % NSEQ, i).start()
 
     recv[i] = send[i]
@@ -257,15 +282,21 @@
         part = (pl.ds(0, NSEQ - 1), pl.ds(0, TOP))
         return rcopy(send.at[part], recv.at[part], a_s, a_r, to_pal)
 
+    slot_all().wait_recv()
     token_all().wait_recv()
 
-    full = iota((NSEQ, CAP, EXT), 1) < TOP
-    came = jnp.where(full, recv[...].astype(F32), 0.0).reshape(NMSG, EXT).astype(BF)
-    one_lane = onehot(iota((8, 128), 1) == 0)
-    slot_row = mm_nt(one_lane, came[:, D:])[0:1]
+    full = iota((NSEQ, CAP, D), 1) < TOP
+    came = jnp.where(full, recv[...].astype(F32), 0.0).reshape(NMSG, D).astype(BF)
+    cells = recv[:, :, 0:128].astype(F32).reshape(NMSG, 128).astype(BF)
+    col = iota((NMSG, NMSG), 1)
+    from_row = onehot(iota((NMSG, NMSG), 0) == (col // CAP) * CAP + TOP)
+    slot_sq = mm_tn(cells, from_row)[0:8]
+    rank_of = iota((8, NMSG), 1) % CAP
+    wanted = (iota((8, NMSG), 0) == rank_of) & (rank_of < TOP)
+    slot_row = jnp.sum(jnp.where(wanted, slot_sq, 0.0), axis=0, keepdims=True)
     placer = onehot((iota((R, NMSG), 0) + 1).astype(F32) == slot_row)
     placer_ref[...] = placer
-    placed = mm(placer, came[:, 0:D]).astype(BF)
+    placed = mm(placer, came).astype(BF)
     pq[g] = placed
 
     def kx_copy(peer, lands):
@@ -439,7 +470,6 @@
 
     att_recv[g] = att_send[g]
 
-    gather_second()
     dq_acc[...] = jnp.zeros((128, QROWS), F32)
 
     def backward(s, n):
@@ -496,21 +526,31 @@
     rs = ring_sum(rs_send, rs_recv, rs_s, rs_r, lambda s, n, part: dkv_acc[n, part], QROWS)
     backward(x2, 3)
     rs[0]()
+    gather_second()
     backward(xp, 2)
     rs[1]()
     backward(xm, 1)
     rs[2]()
     backward(x, 0)
     rs[3]()
-    gather_third()
     dq_rows = jnp.where(half_lanes((QROWS, 128)), dq_acc[...].T * 0.125, 0.0)
     dq3 = dq_rows.reshape(8, R, 128)
-    g_send[:, 64:96] = merge_low(dq3[:, 0:32], dq3[:, 32:64]).astype(BF)
-    dkv = rs[4]().astype(BF)
-    g_send[:, 0:64] = dkv.reshape(8, R, 128)
+    gq_send[...] = merge_low(dq3[:, 0:32], dq3[:, 32:64]).astype(BF)
+
+    def gq_copy(peer, lands):
+        return rcopy(gq_send.at[peer], gq_recv.at[lands], gq_s, gq_r, {"seq": x * 8 + peer})
 
     def g_copy(peer, lands):
         return rcopy(g_send.at[peer], g_recv.at[lands], g_s, g_r, {"seq": x * 8 + peer})
+
+    @pl.loop(1, 8)
+    def _(k):
+        gq_copy((g + k) % 8, g).start()
+
+    gq_recv[g] = gq_send[g]
+    gather_third()
+    dkv = rs[4]().astype(BF)
+    g_send[...] = dkv.reshape(8, R, 128)
 
     @pl.loop(1, 8)
     def _(k):
@@ -545,34 +585,53 @@
 
     ws[3]()
 
+    def lane_block(n):
+        return slice(n * 128, n * 128 + 128)
+
+    seven(gq_send, gq_recv, gq_s, gq_r).wait_recv()
+    for blk in range(4):
+        r0 = gq_recv[2 * blk].astype(F32)
+        r1 = gq_recv[2 * blk + 1].astype(F32)
+        gnat[0:32, lane_block(blk)] = merge_low(r0, r1).astype(BF)
+        gnat[32:64, lane_block(blk)] = merge_high(r0, r1).astype(BF)
+    pg_acc[...] = mm_nt(gnat[:, 0:INNER], w_all[:, 0:INNER])
     seven(g_send, g_recv, g_s, g_r).wait_recv()
     for blk in range(4):
         r0 = g_recv[2 * blk].astype(F32)
         r1 = g_recv[2 * blk + 1].astype(F32)
-        q_at, k_at, v_at = blk * 128, blk * 128 + 512, blk * 128 + 1024
-        gnat[0:32, q_at : q_at + 128] = merge_low(r0[64:96], r1[64:96]).astype(BF)
-        gnat[32:64, q_at : q_at + 128] = merge_high(r0[64:96], r1[64:96]).astype(BF)
-        gnat[:, k_at : k_at + 128] = merge_low(r0[0:64], r1[0:64]).astype(BF)
-        gnat[:, v_at : v_at + 128] = merge_high(r0[0:64], r1[0:64]).astype(BF)
+        gnat[:, lane_block(blk + 4)] = merge_low(r0, r1).astype(BF)
+        gnat[:, lane_block(blk + 8)] = merge_high(r0, r1).astype(BF)
+
     def back_copy(h, peer, lands):
         return rcopy(
-            back_send.at[h, peer, pl.ds(0, TOP)],
-            back_recv.at[h, lands, pl.ds(0, TOP)],
-            b_s,
+            back_send[h].at[peer, pl.ds(0, TOP)],
+            back_recv[h].at[lands, pl.ds(0, TOP)],
+            b_s.at[h],
             b_r.at[h],
             {"seq": peer},
         )
 
+    def back_all(h):
+        part = (pl.ds(0, NSEQ - 1), pl.ds(0, TOP))
+        return rcopy(
+            back_send[h].at[part], back_recv[h].at[part], b_s.at[h], b_r.at[h], to_pal
+        )
+
+    def make_back(h):
+        start, size = PARTS[h]
+        cols = slice(start, start + size)
+        grad = pg_acc[:, cols] + mm_nt(gnat[:, INNER:], w_all[cols, INNER:])
+        back = mm_tn(placer_ref[...], grad.astype(BF))
+        back_send[h][...] = back.reshape(NSEQ, CAP, size).astype(BF)
+
     def send_back(h):
-        grad = mm_nt(gnat[...], w_all[h * HALF : h * HALF + HALF, :]).astype(BF)
-        back = mm_tn(placer_ref[...], grad)
-        back_send[h] = back.reshape(NSEQ, CAP, HALF).astype(BF)
-
         @pl.loop(1, NSEQ)
         def _(k):
             back_copy(h, (i + k) % NSEQ, i).start()
 
-        back_recv[h, i] = back_send[h, i]
+        back_recv[h][i] = back_send[h][i]
+
+    make_back(0)
 
     w_sum = ws[4]()
     w_kv = w_sum[0:128].T.reshape(8, 32, 128)
@@ -593,7 +652,9 @@
     w15_recv[g] = w15_send[g]
 
     send_back(0)
+    make_back(1)
     send_back(1)
+    make_back(2)
 
     seven(w15_send, w15_recv, w15_s, w15_r).wait_recv()
     q_blocks, k_blocks, v_blocks = [], [], []
@@ -620,7 +681,11 @@
                 piece = jnp.where(
                     iota((32, 128), 1) < turn, piece, pltpu.roll(blocks[b + 1], turn, 1)
                 )
-        w2_send[n] = piece.astype(BF)
+        tail = piece[24:32]
+        last = jnp.concatenate(
+            [pltpu.roll(tail, 96, 1), pltpu.roll(tail, 64, 1), pltpu.roll(tail, 32, 1)], axis=0
+        )
+        w2_send[n] = jnp.where(iota((24, 128), 1) < width, piece[0:24], last).astype(BF)
 
     def w2_copy(peer, lands):
         return rcopy(w2_send.at[peer], w2_recv.at[lands], w2_s, w2_r, {"clip": peer})
@@ -634,29 +699,39 @@
         w2_copy((j + k) % n_clip, j).start()
 
     w2_recv[j] = w2_send[j]
-
-    some = iota((NSEQ, CAP, HALF), 1) < TOP
-    for h in range(2):
-        part = (pl.ds(0, NSEQ - 1), pl.ds(0, TOP))
-        rcopy(back_send.at[h].at[part], back_recv.at[h].at[part], b_s, b_r.at[h], to_pal).wait_recv()
-        returned = jnp.where(some, back_recv[h].astype(F32), 0.0).reshape(NMSG, HALF)
+    send_back(2)
+
+    for h, (start, size) in enumerate(PARTS):
+        back_all(h).wait_recv()
+        some = iota((NSEQ, CAP, size), 1) < TOP
+        returned = jnp.where(some, back_recv[h][...].astype(F32), 0.0).reshape(NMSG, size)
         patch_rows = mm_tn(picker[...], returned.astype(BF))
-        patch_out[:, h * HALF : h * HALF + HALF] = (patch_rows * count_inv[:, 0:1]).astype(BF)
+        patch_out[:, start : start + size] = (patch_rows * count_inv[:, 0:1]).astype(BF)
 
     stores[1].start()
 
     w2_all().wait_recv()
-    weight_out[...] = jnp.sum(w2_recv[...].astype(F32), axis=0)[:, 0:width]
+    w_rows = jnp.sum(w2_recv[...].astype(F32), axis=0)
+    weight_out[0:24] = w_rows[:, 0:width]
+    lane = iota((8, 128), 1)
+    tail = jnp.where(
+        lane < 32,
+        pltpu.roll(w_rows[0:8], 32, 1),
+        jnp.where(lane < 64, pltpu.roll(w_rows[8:16], 64, 1), pltpu.roll(w_rows[16:24], 96, 1)),
+    )
+    weight_out[24:32] = tail[:, 0:width]
     stores[2].start()
 
+    slot_all().wait_send()
     token_all().wait_send()
-    part = (pl.ds(0, 2), pl.ds(0, NSEQ - 1), pl.ds(0, TOP))
-    rcopy(back_send.at[part], back_recv.at[part], b_s, b_r.at[0], to_pal).wait_send()
+    for h in range(len(PARTS)):
+        back_all(h).wait_send()
     kx_all().wait_send()
     seven(q_send, q_recv, q_s, q_r).wait_send()
     seven(do_send, do_recv, do_s, do_r).wait_send()
     seven(att_send, att_recv, at_s, at_r).wait_send()
     seven(g_send, g_recv, g_s, g_r).wait_send()
+    seven(gq_send, gq_recv, gq_s, gq_r).wait_send()
     seven(w15_send, w15_recv, w15_s, w15_r).wait_send()
     w2_all().wait_send()
     seven(pq, pq, p_s, p_r.at[0]).wait_send()
@@ -667,17 +742,12 @@
         store.wait()
 
 
-def hand_over(att, patch, weight, att_out, patch_out, weight_out, *scratch):
-    bufs, sems = scratch[0:3], scratch[3]
-    trios = tuple(zip((att, patch, weight), bufs, (att_out, patch_out, weight_out)))
-    come = [pltpu.make_async_copy(a, b, sems.at[n]) for n, (a, b, _) in enumerate(trios)]
-    leave = [pltpu.make_async_copy(b, o, sems.at[3 + n]) for n, (_, b, o) in enumerate(trios)]
-    for move in come:
+def hand_over(att, patch, weight, att_out, patch_out, weight_out, sems):
+    pairs = ((patch, patch_out), (att, att_out), (weight, weight_out))
+    moves = [pltpu.make_async_copy(a, b, sems.at[n]) for n, (a, b) in enumerate(pairs)]
+    for move in moves:
         move.start()
-    for n in range(3):
-        come[n].wait()
-        leave[n].start()
-    for move in leave:
+    for move in moves:
         move.wait()
 
 
@@ -694,10 +764,10 @@
         v((R, INNER), BF),
         v((196, D), BF),
         v((32, 3 * INNER // n_clip), F32),
-        v((NSEQ, CAP, EXT), BF),
-        v((NSEQ, CAP, EXT), BF),
-        v((2, NSEQ, CAP, HALF), BF),
-        v((2, NSEQ, CAP, HALF), BF),
+        v((NSEQ, CAP, D), BF),
+        v((NSEQ, CAP, D), BF),
+        *[v((NSEQ, CAP, size), BF) for _, size in PARTS],
+        *[v((NSEQ, CAP, size), BF) for _, size in PARTS],
         v((D, 3 * INNER), BF),
         v((NMSG, 196), BF),
         v((R, NMSG), BF),
@@ -725,22 +795,27 @@
         v((128, QROWS), F32),
         v((6, 256, 128), BF),
         v((6, 256, 128), BF),
-        v((8, 96, 128), BF),
-        v((8, 96, 128), BF),
+        v((8, R, 128), BF),
+        v((8, R, 128), BF),
+        v((8, 32, 128), BF),
+        v((8, 32, 128), BF),
         v((R, 3 * INNER), BF),
+        v((R, D), F32),
         v((4, 192, 256), F32),
         v((6, 96, 256), BF),
         v((6, 96, 256), BF),
         v((8, 48, 128), BF),
         v((8, 48, 128), BF),
-        v((n_clip, 32, 128), BF),
-        v((n_clip, 32, 128), BF),
+        v((n_clip, 24, 128), BF),
+        v((n_clip, 24, 128), BF),
         dma((6,)),
         dma((3,)),
         dma,
         dma,
         dma,
-        dma((2,)),
+        dma,
+        dma((3,)),
+        dma((3,)),
         dma,
         dma((13,)),
         dma,
@@ -755,6 +830,8 @@
         dma,
         dma,
         dma((6,)),
+        dma,
+        dma,
         dma,
         dma,
         dma,
@@ -770,6 +847,7 @@
         jax.ShapeDtypeStruct((1, 196, D), BF),
         jax.ShapeDtypeStruct((32, 3 * INNER // n_clip), F32),
     )
+    operands = (patches, segment, dest_shard, dest_slot, w_qkv, out_grad)
     results = pl.pallas_call(
         functools.partial(kernel, n_clip),
         out_shape=shapes,
@@ -777,16 +855,17 @@
         out_specs=(anywhere,) * 3,
         scratch_shapes=scratch,
         compiler_params=pltpu.CompilerParams(
-            collective_id=0, has_side_effects=True, vmem_limit_bytes=67_043_328
+            collective_id=0, has_side_effects=True, vmem_limit_bytes=40 * 1024 * 1024
         ),
         name="rebalance_attention",
-    )(patches, segment, dest_shard, dest_slot, w_qkv, out_grad)
+    )(*[pltpu.with_memory_space_constraint(a, pltpu.HBM) for a in operands])
     return pl.pallas_call(
         hand_over,
         out_shape=shapes,
         in_specs=[anywhere] * 3,
         out_specs=(anywhere,) * 3,
-        scratch_shapes=[v(t.shape, t.dtype) for t in shapes] + [dma((6,))],
+        scratch_shapes=[dma((3,))],
+        compiler_params=pltpu.CompilerParams(vmem_limit_bytes=2 * 1024 * 1024),
         name="hand_over",
     )(*results)
 

time: 79.7 us -> 77.8 us (0.976)
  Pallas kernels: 78.6 us -> 77.1 us
    pallas_call x1, Pallas kernels: 1.85 us -> 0.8 us  [local(): pl.pallas_call(hand_over, out_shape=shapes, in_specs=[anywhere] * 3, out_...]
where the time goes in v4:
time: 77.8 us; the launch traced here: 77.7 us
  Pallas kernels  77.1 us (99%)
    pallas_call x1, Pallas kernels, local(): pl.pallas_call(functools.partial(kernel, n_clip), out_shape=shapes, in_sp...  76.3 us

profile of v4, /device:TPU:1, one launch (start us, length us, event | category | flops | bytes accessed | tf_op | source)
XLA Modules:
  0.0 77.7 jit_solution(13257393712584529372)
XLA Ops:
  0.6 76.3 %rebalance_attention.1 = (bf16[1,64,512]{2,1,0:T(8,128)(2,1)S(1)}, bf16[1,196,1024]{2,1,0:T(8,128)(2,1)S(1)}, f32[32,96]{1,0:T(8,128)S(1)}) custom-call(bf16[1,196,1024]{2,1,0:T(8,128)(2,1)} %patches_hbm.1, s32[1,196]{1,0:T(1,128)} %segment_hbm.1, s32[1,192]{1,0:T(1,128)} %shard_hbm.1, s32[1,192]{1,0:T(1,128)} %slot_hbm.1, bf16[1024,1536]{1,0:T(8,128)(2,1)} %w_hbm.1, ...), custom_call_target="tpu_custom_call" | custom-call | tf_op jit(solution)/shard_map/rebalance_attention/pallas_call | solution.py:851
  76.9 0.8 %hand_over.1 = (bf16[1,64,512]{2,1,0:T(8,128)(2,1)}, bf16[1,196,1024]{2,1,0:T(8,128)(2,1)}, f32[32,96]{1,0:T(8,128)}) custom-call(bf16[1,64,512]{2,1,0:T(8,128)(2,1)S(1)} %get-tuple-element.6.att, bf16[1,196,1024]{2,1,0:T(8,128)(2,1)S(1)} %get-tuple-element.7.patch, f32[32,96]{1,0:T(8,128)S(1)} %get-tuple-element.8.weight), custom_call_target="tpu_custom_call" | custom-call | tf_op jit(solution)/shard_map/hand_over/pallas_call | solution.py:862

commit v5 on v4

--- a/solution.py
+++ b/solution.py
@@ -21,7 +21,13 @@
 QROWS = 512
 QC = 256
 TOP = 6
-PARTS = ((0, 512), (512, 384), (896, 128))
+PARTS = ((0, 256), (256, 512), (768, 256))
+HOPS_X = (0, 1, 2, 1)
+HOPS_Y = (0, 2, 4, 2)
+FAR_FIRST = sorted(
+    ((a, b, d) for a in range(4) for b in range(4) for d in range(2) if a or b or d),
+    key=lambda t: -(HOPS_X[t[0]] + HOPS_Y[t[1]]),
+)
 
 
 def iota(shape, dim):
@@ -174,6 +180,12 @@
     def seq_dev(dx, dy, dc):
         return {"seq": dx * 8 + dy * 2 + dc}
 
+    xs = (x, xp, x2, xm)
+    ys = (y, yp, y2, ym)
+    cs = (c, 1 - c)
+    clip_peers = [xs[a] * 8 + ys[b] * 2 + cs[d] for a, b, d in FAR_FIRST]
+    group_peers = [ys[b] * 2 + cs[d] for a, b, d in FAR_FIRST if a == 0]
+
     def rcopy(src, dst, ss, rs, dev):
         return pltpu.make_async_remote_copy(
             src_ref=src, dst_ref=dst, send_sem=ss, recv_sem=rs, device_id=dev, device_id_type=MESH
@@ -196,16 +208,15 @@
         load.start()
 
     to_pal = seq_dev(x, y, 1 - c)
+    h_g = y * 2 + 1 - c
 
     def seven(src, dst, ss, rs):
         return rcopy(src.at[pl.ds(0, 7)], dst.at[pl.ds(0, 7)], ss, rs, to_pal)
 
     barrier = pltpu.get_barrier_semaphore()
 
-    for k in range(1, NSEQ):
-        pl.semaphore_signal(
-            barrier, inc=1, device_id={"seq": lax.rem(i + k, NSEQ)}, device_id_type=MESH
-        )
+    for peer in clip_peers:
+        pl.semaphore_signal(barrier, inc=1, device_id={"seq": peer}, device_id_type=MESH)
     for k in range(1, n_clip):
         pl.semaphore_signal(
             barrier, inc=1, device_id={"clip": lax.rem(j + k, n_clip)}, device_id_type=MESH
@@ -260,10 +271,9 @@
             {"seq": peer},
         )
 
-    @pl.loop(1, NSEQ)
-    def _(k):
-        slot_copy((i + k) % NSEQ, i).start()
-        token_copy((i + k) % NSEQ, i).start()
+    for peer in clip_peers:
+        slot_copy(peer, i).start()
+        token_copy(peer, i).start()
 
     recv[i] = send[i]
 
@@ -317,32 +327,30 @@
     def half_up(v):
         return v.astype(BF).astype(F32)
 
-    proj = half_up(mm(placed, w_all[:, INNER:]))
-    for blk in range(4):
-        k_blk = proj[:, blk * 128 : blk * 128 + 128]
-        v_blk = proj[:, INNER + blk * 128 : INNER + blk * 128 + 128]
-        kv_send[2 * blk] = merge_low(k_blk, v_blk).astype(BF)
-        kv_send[2 * blk + 1] = merge_high(k_blk, v_blk).astype(BF)
-
-    @pl.loop(1, 8)
-    def _(k):
-        kx_copy((g + k) % 8, g).start()
-
+    def w_cols(at, pair):
+        return w_all[:, pl.ds(pl.multiple_of(at + pair * 128, 128), 128)]
+
+    for pair in (y2, yp, ym, y):
+        w_pair = jnp.concatenate([w_cols(INNER, pair), w_cols(2 * INNER, pair)], axis=1)
+        proj = half_up(mm(placed, w_pair))
+        k_blk, v_blk = proj[:, 0:128], proj[:, 128:256]
+        kv_send[2 * pair] = merge_low(k_blk, v_blk).astype(BF)
+        kv_send[2 * pair + 1] = merge_high(k_blk, v_blk).astype(BF)
+        if pair is y:
+            kx_copy(h_g, g).start()
+        else:
+            kx_copy(2 * pair + c, g).start()
+            kx_copy(2 * pair + 1 - c, g).start()
     kv[x, pl.ds(pl.multiple_of(g * R, R), R)] = kv_send[g]
     proj_q = half_up(mm(placed, w_all[:, 0:INNER])) * 0.125
     for blk in range(4):
         q_blk = proj_q[:, blk * 128 : blk * 128 + 128]
         q_send[2 * blk] = merge_low(q_blk[0:32], q_blk[32:64]).astype(BF)
         q_send[2 * blk + 1] = merge_high(q_blk[0:32], q_blk[32:64]).astype(BF)
-
-    @pl.loop(1, 8)
-    def _(k):
-        q_copy((g + k) % 8, g).start()
-
-    @pl.loop(1, 8)
-    def _(k):
-        do_copy((g + k) % 8, g).start()
-
+    for peer in group_peers:
+        q_copy(peer, g).start()
+    for peer in group_peers:
+        do_copy(peer, g).start()
     q_recv[g] = q_send[g]
     do_recv[g] = do_send[g]
 
@@ -354,7 +362,7 @@
         ref = pq.at[s] if half is None else pq.at[s, half]
         return rcopy(ref, ref, p_s, p_r.at[n], dev)
 
-    h_p, h_m, h_2, h_g = yp * 2 + 1 - c, ym * 2 + 1 - c, y2 * 2 + 1 - c, y * 2 + 1 - c
+    h_p, h_m, h_2 = yp * 2 + 1 - c, ym * 2 + 1 - c, y2 * 2 + 1 - c
 
     def gather_first():
         p_copy(0, g, A, to_yp).start()
@@ -464,9 +472,8 @@
     def at_copy(peer, lands):
         return rcopy(att_send.at[peer], att_recv.at[lands], at_s, at_r, {"seq": x * 8 + peer})
 
-    @pl.loop(1, 8)
-    def _(k):
-        at_copy((g + k) % 8, g).start()
+    for peer in group_peers:
+        at_copy(peer, g).start()
 
     att_recv[g] = att_send[g]
 
@@ -543,18 +550,16 @@
     def g_copy(peer, lands):
         return rcopy(g_send.at[peer], g_recv.at[lands], g_s, g_r, {"seq": x * 8 + peer})
 
-    @pl.loop(1, 8)
-    def _(k):
-        gq_copy((g + k) % 8, g).start()
+    for peer in group_peers:
+        gq_copy(peer, g).start()
 
     gq_recv[g] = gq_send[g]
     gather_third()
     dkv = rs[4]().astype(BF)
     g_send[...] = dkv.reshape(8, R, 128)
 
-    @pl.loop(1, 8)
-    def _(k):
-        g_copy((g + k) % 8, g).start()
+    for peer in group_peers:
+        g_copy(peer, g).start()
 
     g_recv[g] = g_send[g]
 
@@ -625,13 +630,13 @@
         back_send[h][...] = back.reshape(NSEQ, CAP, size).astype(BF)
 
     def send_back(h):
-        @pl.loop(1, NSEQ)
-        def _(k):
-            back_copy(h, (i + k) % NSEQ, i).start()
+        for peer in clip_peers:
+            back_copy(h, peer, i).start()
 
         back_recv[h][i] = back_send[h][i]
 
     make_back(0)
+    send_back(0)
 
     w_sum = ws[4]()
     w_kv = w_sum[0:128].T.reshape(8, 32, 128)
@@ -645,13 +650,11 @@
             w15_send.at[peer], w15_recv.at[lands], w15_s, w15_r, {"seq": x * 8 + peer}
         )
 
-    @pl.loop(1, 8)
-    def _(k):
-        w15_copy((g + k) % 8, g).start()
+    for peer in group_peers:
+        w15_copy(peer, g).start()
 
     w15_recv[g] = w15_send[g]
 
-    send_back(0)
     make_back(1)
     send_back(1)
     make_back(2)

time: 77.8 us -> 76.3 us (0.981)
  Pallas kernels: 77.1 us -> 75.1 us
    pallas_call x1, Pallas kernels: 76.3 us -> 74.3 us  [local(): pl.pallas_call(functools.partial(kernel, n_clip), out_shape=shapes, in_sp...]
where the time goes in v5:
time: 76.3 us; the launch traced here: 75.8 us
  Pallas kernels  75.1 us (98%)
    pallas_call x1, Pallas kernels, local(): pl.pallas_call(functools.partial(kernel, n_clip), out_shape=shapes, in_sp...  74.3 us

profile of v5, /device:TPU:1, one launch (start us, length us, event | category | flops | bytes accessed | tf_op | source)
XLA Modules:
  0.0 75.8 jit_solution(15426834500890974638)
XLA Ops:
  0.6 74.3 %rebalance_attention.1 = (bf16[1,64,512]{2,1,0:T(8,128)(2,1)S(1)}, bf16[1,196,1024]{2,1,0:T(8,128)(2,1)S(1)}, f32[32,96]{1,0:T(8,128)S(1)}) custom-call(bf16[1,196,1024]{2,1,0:T(8,128)(2,1)} %patches_hbm.1, s32[1,196]{1,0:T(1,128)} %segment_hbm.1, s32[1,192]{1,0:T(1,128)} %shard_hbm.1, s32[1,192]{1,0:T(1,128)} %slot_hbm.1, bf16[1024,1536]{1,0:T(8,128)(2,1)} %w_hbm.1, ...), custom_call_target="tpu_custom_call" | custom-call | tf_op jit(solution)/shard_map/rebalance_attention/pallas_call | solution.py:854
  75.0 0.8 %hand_over.1 = (bf16[1,64,512]{2,1,0:T(8,128)(2,1)}, bf16[1,196,1024]{2,1,0:T(8,128)(2,1)}, f32[32,96]{1,0:T(8,128)}) custom-call(bf16[1,64,512]{2,1,0:T(8,128)(2,1)S(1)} %get-tuple-element.6.att, bf16[1,196,1024]{2,1,0:T(8,128)(2,1)S(1)} %get-tuple-element.7.patch, f32[32,96]{1,0:T(8,128)S(1)} %get-tuple-element.8.weight), custom_call_target="tpu_custom_call" | custom-call | tf_op jit(solution)/shard_map/hand_over/pallas_call | solution.py:865

commit v6 on v5

--- a/solution.py
+++ b/solution.py
@@ -21,7 +21,7 @@
 QROWS = 512
 QC = 256
 TOP = 6
-PARTS = ((0, 256), (256, 512), (768, 256))
+PARTS = ((0, 256), (256, 640), (896, 128))
 HOPS_X = (0, 1, 2, 1)
 HOPS_Y = (0, 2, 4, 2)
 FAR_FIRST = sorted(
@@ -588,8 +588,6 @@
         att_out[32:64, lanes] = merge_high(a0, a1).astype(BF)
     stores[0].start()
 
-    ws[3]()
-
     def lane_block(n):
         return slice(n * 128, n * 128 + 128)
 
@@ -600,6 +598,9 @@
         gnat[0:32, lane_block(blk)] = merge_low(r0, r1).astype(BF)
         gnat[32:64, lane_block(blk)] = merge_high(r0, r1).astype(BF)
     pg_acc[...] = mm_nt(gnat[:, 0:INNER], w_all[:, 0:INNER])
+
+    ws[3]()
+
     seven(g_send, g_recv, g_s, g_r).wait_recv()
     for blk in range(4):
         r0 = g_recv[2 * blk].astype(F32)

time: 76.3 us -> 76.6 us (level)
  no operation moved by 1% of the time
where the time goes in v6:
time: 76.6 us; the launch traced here: 76.4 us
  Pallas kernels  75.8 us (99%)
    pallas_call x1, Pallas kernels, local(): pl.pallas_call(functools.partial(kernel, n_clip), out_shape=shapes, in_sp...  75 us

profile of v6, /device:TPU:1, one launch (start us, length us, event | category | flops | bytes accessed | tf_op | source)
XLA Modules:
  0.0 76.4 jit_solution(5400298445499975034)
XLA Ops:
  0.6 75.0 %rebalance_attention.1 = (bf16[1,64,512]{2,1,0:T(8,128)(2,1)S(1)}, bf16[1,196,1024]{2,1,0:T(8,128)(2,1)S(1)}, f32[32,96]{1,0:T(8,128)S(1)}) custom-call(bf16[1,196,1024]{2,1,0:T(8,128)(2,1)} %patches_hbm.1, s32[1,196]{1,0:T(1,128)} %segment_hbm.1, s32[1,192]{1,0:T(1,128)} %shard_hbm.1, s32[1,192]{1,0:T(1,128)} %slot_hbm.1, bf16[1024,1536]{1,0:T(8,128)(2,1)} %w_hbm.1, ...), custom_call_target="tpu_custom_call" | custom-call | tf_op jit(solution)/shard_map/rebalance_attention/pallas_call | solution.py:855
  75.6 0.8 %hand_over.1 = (bf16[1,64,512]{2,1,0:T(8,128)(2,1)}, bf16[1,196,1024]{2,1,0:T(8,128)(2,1)}, f32[32,96]{1,0:T(8,128)}) custom-call(bf16[1,64,512]{2,1,0:T(8,128)(2,1)S(1)} %get-tuple-element.6.att, bf16[1,196,1024]{2,1,0:T(8,128)(2,1)S(1)} %get-tuple-element.7.patch, f32[32,96]{1,0:T(8,128)S(1)} %get-tuple-element.8.weight), custom_call_target="tpu_custom_call" | custom-call | tf_op jit(solution)/shard_map/hand_over/pallas_call | solution.py:866
